TPU v7x, 32 devices: a whole 2x2x4 slice. The times are simulated.
32 devices in a mesh: tm: 8 (over z, y), tensor: 4 (over x, core).
Axes of the slice: x: 2, y: 2, z: 4, core: 2. Of those that a mesh axis runs over, the one named last changes fastest.
Arguments:
- frames_in: bfloat16 [8, 1024, 768], P('tm'), may hold values from -16 to 16
- norm_gain: float32 [768], replicated, may hold values from 0.1 to 1.9
- w_qkv: bfloat16 [768, 3, 768], P(None, None, 'tensor'), may hold values from -0.21650635 to 0.21650635
- w_out: bfloat16 [768, 768], P('tensor'), may hold values from -0.21875 to 0.21875
- keep_runs: int32 [8, 16, 2], replicated, may hold values from 0 to 1023, as said below
- out_cotangent: bfloat16 [8, 1024, 768], P('tm'), may hold values from -6 to 6
Outputs:
- block_out: bfloat16 [8, 1024, 768], P('tm', None, 'tensor')
- grad_in: bfloat16 [8, 1024, 768], P('tm', None, 'tensor')
- grad_qkv: bfloat16 [768, 3, 768], P('tm', None, 'tensor')
- grad_proj: bfloat16 [768, 768], P('tensor', 'tm')
- grad_gain: float32 [768], P('tensor')
Inputs may be any that keep to these rules, and one draw needn't show every extreme that they name: keep_runs[t, r] = (first, length) is the r-th run of kept positions of frame t; the 16 runs of a frame are disjoint, in rising order, and lie within the frame's 1024 positions.
All inputs are finite; a program needn't handle non-finite values.
Results may differ from a plain program's by a relative error of at most 0.034.
Values may be sent and summed in bfloat16 or wider, within the bound.
No kernel may reach another device: no remote copies, remote signals or barrier semaphores. Data moves between devices by JAX's collectives and lax.ppermute only.
A program may use at most 128 MiB of HBM per device.

v0:
```python
import jax
import jax.numpy as jnp
from jax import lax
from jax.sharding import PartitionSpec as P

D = 768
H = 12


epsilon = 1e-05


def kept_table(keep_runs, first_place, place_count):
    places = first_place + jnp.arange(place_count, dtype=jnp.int32)
    starts = keep_runs[:, :, 0:1]
    lengths = keep_runs[:, :, 1:2]
    inside = (places[None, None, :] >= starts) & (places[None, None, :] < starts + lengths)
    return jnp.sum(inside.astype(jnp.int32), axis=1)


def normalize(frames_in):
    frames_float = frames_in.astype(jnp.float32)
    centre = jnp.mean(frames_float, axis=-1, keepdims=True)
    shifted = frames_float - centre
    spread = jnp.mean(shifted * shifted, axis=-1, keepdims=True)
    inverse_spread = lax.rsqrt(spread + epsilon)
    return (frames_float, shifted * inverse_spread, inverse_spread)


def attend(packed, kept_mask):
    frames, places, row_width = packed.shape
    head_width = D // H
    pieces = packed.reshape(frames, places, 3, row_width // (3 * head_width), head_width)
    scores = jnp.einsum(
        "tphd,uphd->phtu", pieces[:, :, 0], pieces[:, :, 1], preferred_element_type=jnp.float32
    )
    scores = scores * head_width ** (-0.5)
    allowed = jnp.transpose(kept_mask)[:, None, None, :] > 0
    scores = jnp.where(allowed, scores, -1000000000.0)
    row_max = jnp.max(scores, axis=-1, keepdims=True)
    exponent = jnp.exp(scores - row_max)
    weights = (exponent / jnp.sum(exponent, axis=-1, keepdims=True)).astype(jnp.bfloat16)
    mixed_rows = jnp.einsum(
        "phtu,uphd->tphd", weights, pieces[:, :, 2], preferred_element_type=jnp.float32
    )
    mixed_rows = jnp.where(kept_mask[:, :, None, None] > 0, mixed_rows, 0.0)
    return mixed_rows.astype(jnp.bfloat16).reshape(frames, places, row_width // 3)


def project(rows_in, weight):
    leading = rows_in.shape[:-1]
    flat = jnp.dot(
        rows_in.reshape(-1, rows_in.shape[-1]), weight, preferred_element_type=jnp.float32
    )
    return flat.astype(jnp.bfloat16).reshape(leading + (weight.shape[1],))


def contract_rows(left, right):
    return lax.dot_general(
        left.reshape(-1, left.shape[-1]),
        right.reshape(-1, right.shape[-1]),
        (((0,), (0,)), ((), ())),
        preferred_element_type=jnp.float32,
    )


def back_project(cotangent, weight):
    leading = cotangent.shape[:-1]
    flat = lax.dot_general(
        cotangent.reshape(-1, cotangent.shape[-1]),
        weight,
        (((1,), (1,)), ((), ())),
        preferred_element_type=jnp.float32,
    )
    return flat.reshape(leading + (weight.shape[0],))


def body(frames_in, norm_gain, w_qkv, w_out, keep_runs, out_cotangent):
    frames_here, place_total, row_width = frames_in.shape
    places_here = place_total // lax.axis_size("tm")
    width_share = row_width // lax.axis_size("tensor")
    share_start = lax.axis_index("tensor") * width_share
    channels = w_qkv.shape[2]
    w_flat = w_qkv.reshape(row_width, 3 * channels)
    kept_mask = kept_table(keep_runs, lax.axis_index("tm") * places_here, places_here)
    frames_float, standard, inverse_spread = normalize(frames_in)
    normed = (standard * norm_gain).astype(jnp.bfloat16)
    packed = project(normed, w_flat)
    packed_places = lax.all_to_all(packed, "tm", split_axis=1, concat_axis=0, tiled=True)

    def attend_here(packed_arg):
        return attend(packed_arg, kept_mask)

    mixed_places, attend_back = jax.vjp(attend_here, packed_places)
    mixed_frames = lax.all_to_all(mixed_places, "tm", split_axis=0, concat_axis=1, tiled=True)
    branch = jnp.dot(mixed_frames.reshape(-1, channels), w_out, preferred_element_type=jnp.float32)
    branch = branch.reshape(frames_here, place_total, row_width)
    branch_share = lax.psum_scatter(
        branch.astype(jnp.bfloat16), "tensor", scatter_dimension=2, tiled=True
    ).astype(jnp.float32)
    residual_share = lax.dynamic_slice_in_dim(frames_float, share_start, width_share, 2)
    block_out = (residual_share + branch_share).astype(jnp.bfloat16)
    proj_part = contract_rows(mixed_frames, out_cotangent)
    grad_proj = lax.psum_scatter(proj_part, "tm", scatter_dimension=1, tiled=True).astype(
        jnp.bfloat16
    )
    mixed_cot = back_project(out_cotangent, w_out).astype(jnp.bfloat16)
    mixed_cot_places = lax.all_to_all(mixed_cot, "tm", split_axis=1, concat_axis=0, tiled=True)
    packed_cot_places = attend_back(mixed_cot_places)[0]
    gain_share = lax.dynamic_slice_in_dim(norm_gain, share_start, width_share, 0)
    standard_share = lax.dynamic_slice_in_dim(standard, share_start, width_share, 2)
    packed_cot = lax.all_to_all(packed_cot_places, "tm", split_axis=0, concat_axis=1, tiled=True)
    qkv_part = contract_rows(normed, packed_cot)
    normed_part = back_project(packed_cot, w_flat)
    whole_cot = lax.psum(normed_part.astype(jnp.bfloat16), "tensor").astype(jnp.float32)
    whole_cot = lax.optimization_barrier(whole_cot.astype(jnp.bfloat16)).astype(jnp.float32)
    scaled_whole = whole_cot * norm_gain
    mean_plain = jnp.mean(scaled_whole, axis=-1, keepdims=True)
    mean_cross = jnp.mean(scaled_whole * standard, axis=-1, keepdims=True)
    cot_share = lax.dynamic_slice_in_dim(whole_cot, share_start, width_share, 2)
    scaled_share = cot_share * gain_share
    through = inverse_spread * (scaled_share - mean_plain - standard_share * mean_cross)
    gain_part = jnp.sum(cot_share * standard_share, axis=(0, 1))
    cot_share_out = lax.dynamic_slice_in_dim(out_cotangent, share_start, width_share, 2).astype(
        jnp.float32
    )
    grad_in = (cot_share_out + through).astype(jnp.bfloat16)
    grad_qkv = lax.psum_scatter(
        qkv_part.reshape(row_width, 3, channels), "tm", scatter_dimension=0, tiled=True
    ).astype(jnp.bfloat16)
    grad_gain = lax.psum(gain_part, "tm")
    return (block_out, grad_in, grad_qkv, grad_proj, grad_gain)


def solution(mesh):
    in_specs = (
        P("tm", None, None),
        P(),
        P(None, None, "tensor"),
        P("tensor", None),
        P(),
        P("tm", None, None),
    )
    out_specs = (
        P("tm", None, "tensor"),
        P("tm", None, "tensor"),
        P("tm", None, "tensor"),
        P("tensor", "tm"),
        P("tensor"),
    )
    return jax.shard_map(body, mesh=mesh, in_specs=in_specs, out_specs=out_specs, check_vma=False)
```

profile of v0, /device:TPU:0, one launch (start us, length us, event | category | flops | bytes accessed | tf_op | source)
XLA Modules:
  0.0 338.7 jit_solution(6467486779215469923)
XLA Ops:
  11.6 4.9 %reduce.4 = bf16[1024,192]{1,0:T(8,128)(2,1)} reduce(bf16[1024,1,192]{2,1,0:T(2,128)(2,1)S(1)} %bitcast.147, bf16[]{:T(256)} %broadcast.97), dimensions={1}, to_apply=%bitcast.110.reduce_sub_computation | reduce | bytes 786434
  18.9 7.7 %all-to-all-start.2 = ((bf16[8,2,12288]{2,1,0:T(2,128)(2,1)}), bf16[8,2,12288]{2,1,0:T(2,128)(2,1)S(1)}, u32[]{:S(2)}, u32[]{:S(2)}) async-start(bf16[8,2,12288]{2,1,0:T(2,128)(2,1)} %reshape.160), calls=%async_computation.2 | async-start | bytes 786432 | tf_op jit(solution)/shard_map/all_to_all | solution.py:108
  29.9 6.2 %copy.106 = bf16[1,1024,576]{2,0,1:T(2,128)(2,1)} copy(bf16[1,1024,576]{1,2,0:T(8,128)(2,1)} %fusion.17) | data formatting | bytes 2359296 | tf_op jit(solution)/shard_map/reshape | solution.py:55
  36.1 11.0 %reduce.5 = bf16[1024,576]{1,0:T(8,128)(2,1)} reduce(bf16[1024,1,576]{2,1,0:T(2,128)(2,1)} %bitcast.141, bf16[]{:T(256)} %broadcast.97), dimensions={1}, to_apply=%bitcast.108.reduce_sub_computation | reduce | bytes 2359298
  47.1 4.4 %reshape.158 = bf16[8,2,36864]{2,1,0:T(2,128)(2,1)} reshape(bf16[1024,576]{1,0:T(8,128)(2,1)} %reduce.5) | data formatting | bytes 2359296
  51.5 17.1 %all-to-all-start = ((bf16[8,2,36864]{2,1,0:T(2,128)(2,1)}), bf16[8,2,36864]{2,1,0:T(2,128)(2,1)}, u32[]{:S(2)}, u32[]{:S(2)}) async-start(bf16[8,2,36864]{2,1,0:T(2,128)(2,1)} %reshape.158), calls=%async_computation | async-start | bytes 2359296 | tf_op jit(solution)/shard_map/all_to_all | solution.py:89
  74.9 22.0 %all-to-all-done = bf16[8,2,36864]{2,1,0:T(2,128)(2,1)} async-done(((bf16[8,2,36864]{2,1,0:T(2,128)(2,1)}), bf16[8,2,36864]{2,1,0:T(2,128)(2,1)}, u32[]{:S(2)}, u32[]{:S(2)}) %all-to-all-start) | async-done | bytes 1179680 | tf_op jit(solution)/shard_map/all_to_all | solution.py:89
  96.9 6.5 %reshape.159 = bf16[1024,1,576]{2,1,0:T(2,128)(2,1)} reshape(bf16[8,2,36864]{2,1,0:T(2,128)(2,1)} %all-to-all-done) | data formatting | bytes 2359296
  103.4 6.0 %copy.107 = bf16[1,1024,576]{1,2,0:T(8,128)(2,1)} copy(bf16[1,1024,576]{2,0,1:T(2,128)(2,1)} %bitcast.142) | data formatting | bytes 2359296 | tf_op jit(solution)/shard_map/all_to_all | solution.py:89
  113.6 2.7 copy.137
  128.4 3.5 %all-to-all-start.1 = ((bf16[8,128,192]{1,2,0:T(8,128)(2,1)}), bf16[8,128,192]{1,2,0:T(8,128)(2,1)S(1)}, u32[]{:S(2)}, u32[]{:S(2)}) async-start(bf16[8,128,192]{1,2,0:T(8,128)(2,1)} %bitcast.149), calls=%async_computation.1 | async-start | bytes 786432 | tf_op jit(solution)/shard_map/all_to_all | solution.py:95
  134.1 3.7 %convert_reduce_fusion.1 = (f32[128,3,8]{2,1,0:T(4,128)S(1)}, pred[128,3,8,8]{2,3,1,0:T(8,128)(4,1)S(1)}, f32[128,3,8]{2,1,0:T(4,128)S(1)}, bf16[128,3,8,8]{2,3,1,0:T(8,128)(2,1)S(1)}) fusion(f32[128,3,8,8]{2,3,1,0:T(8,128)} %copy-done.2, f32[128,3,8]{2,1,0:T(4,128)S(1)} %get-tuple-element.57, f32[128,3,8]{2,1,0:T(4,128)} %multiply_divide_fusion, ...), kind=kOutput, calls=%fused_computation.25 | convolution fusion | flops 3336192 | bytes 1007616 | tf_op jit(solution)/shard_map/transpose(jvp(phtu,uphd->tphd))/dot_general | solution.py:43
  143.9 4.0 %copy.121 = bf16[8,128,3,3,64]{1,4,3,2,0:T(8,128)(2,1)} copy(bf16[8,128,3,3,64]{4,0,3,1,2:T(8,128)(2,1)} %pad_add_fusion) | data formatting | bytes 2359296 | tf_op jit(solution)/shard_map/transpose(jvp())/add_any | solution.py:35
  147.9 6.0 %all-to-all-start.3 = ((bf16[8,128,576]{1,2,0:T(8,128)(2,1)}), bf16[8,128,576]{1,2,0:T(8,128)(2,1)}, u32[]{:S(2)}, u32[]{:S(2)}) async-start(bf16[8,128,576]{1,2,0:T(8,128)(2,1)} %bitcast.144), calls=%async_computation.3 | async-start | bytes 2359296 | tf_op jit(solution)/shard_map/all_to_all | solution.py:112
  153.9 3.0 fusion.23
  157.0 28.6 %all-to-all-done.3 = bf16[8,128,576]{1,2,0:T(8,128)(2,1)} async-done(((bf16[8,128,576]{1,2,0:T(8,128)(2,1)}), bf16[8,128,576]{1,2,0:T(8,128)(2,1)}, u32[]{:S(2)}, u32[]{:S(2)}) %all-to-all-start.3) | async-done | bytes 1179680 | tf_op jit(solution)/shard_map/all_to_all | solution.py:112
  185.6 3.9 %fusion.16 = bf16[1,1024,768]{2,1,0:T(8,128)(2,1)} fusion(bf16[768,576]{0,1:T(8,128)(2,1)S(1)} %bitcast.139, bf16[8,128,576]{1,2,0:T(8,128)(2,1)} %all-to-all-done.3), kind=kOutput, calls=%fused_computation.31 | convolution fusion | flops 906756096 | bytes 3637248 | tf_op jit(solution)/shard_map/dot_general | solution.py:69
  192.2 8.5 %copy.130 = bf16[1,1024,768]{1,0,2:T(2,128)(2,1)} copy(bf16[1,1024,768]{2,1,0:T(8,128)(2,1)} %fusion.15) | data formatting | bytes 3145728
  200.7 3.7 %copy.158 = bf16[768,1,1024]{2,0,1:T(8,128)(2,1)} copy(bf16[768,1,1024]{2,1,0:T(2,128)(2,1)} %bitcast.140) | data formatting | bytes 3145728
  206.1 3.3 fusion.4
  211.4 15.4 %reduce-scatter.12.cloned.1.call-done = f32[96,192]{1,0:T(8,128)} async-done(((f32[768,192]{1,0:T(8,128)}), f32[96,192]{1,0:T(8,128)}) %reduce-scatter.12.cloned.1.call-update) | async-done | bytes 73744
  228.4 3.5 %all-reduce.5.cloned.1.call-done = bf16[1,1024,768]{2,1,0:T(8,128)(2,1)} async-done(((bf16[1,1024,768]{2,1,0:T(8,128)(2,1)}), bf16[1,1024,768]{2,1,0:T(8,128)(2,1)}) %all-reduce.5.cloned.1.call-update) | async-done | bytes 1572880 | tf_op jit(solution)/shard_map/psum | solution.py:115
  238.5 21.8 %psum.15 = f32[192]{0:T(256)} all-reduce(f32[192]{0:T(256)S(1)} %get-tuple-element.46), channel_id=1, replica_groups=mesh['tm'=8,'tensor'=4] {'tm'}, use_global_device_ids=true, to_apply=%region_15.16 | all-reduce | flops 192 | bytes 1536 | tf_op jit(solution)/shard_map/psum | solution.py:131
  265.6 64.1 %reduce-scatter.8.cloned.1.call-done = f32[96,3,192]{2,0,1:T(8,128)} async-done(((f32[768,3,192]{2,0,1:T(8,128)}), f32[96,3,192]{2,0,1:T(8,128)}) %reduce-scatter.8.cloned.1.call-update) | async-done | bytes 221200 | tf_op jit(solution)/shard_map/reduce_scatter | solution.py:128
  (93 shorter events, 61.4 us)
Async XLA Ops:
  8.0 19.6 %copy-start = (bf16[768,3,192]{0,2,1:T(8,128)(2,1)S(1)}, bf16[768,3,192]{0,2,1:T(8,128)(2,1)}, u32[]{:S(2)}) copy-start(bf16[768,3,192]{0,2,1:T(8,128)(2,1)} %param.8) | copy-start | bytes 2654212
  11.6 15.1 %copy-start.1 = (bf16[1,1024,768]{2,1,0:T(8,128)(2,1)S(1)}, bf16[1,1024,768]{2,1,0:T(8,128)(2,1)}, u32[]{:S(2)}) copy-start(bf16[1,1024,768]{2,1,0:T(8,128)(2,1)} %param.6) | copy-start | bytes 4718596
  18.9 32.6 %all-to-all-start.2 = ((bf16[8,2,12288]{2,1,0:T(2,128)(2,1)}), bf16[8,2,12288]{2,1,0:T(2,128)(2,1)S(1)}, u32[]{:S(2)}, u32[]{:S(2)}) async-start(bf16[8,2,12288]{2,1,0:T(2,128)(2,1)} %reshape.160), calls=%async_computation.2 | async-start | bytes 786432 | tf_op jit(solution)/shard_map/all_to_all | solution.py:108
  26.7 0.9 copy-start.14
  51.5 17.2 %copy-start.13 = (s32[8,16,2]{1,2,0:T(2,128)S(1)}, s32[8,16,2]{1,2,0:T(2,128)}, u32[]{:S(2)}) copy-start(s32[8,16,2]{1,2,0:T(2,128)} %param.10) | copy-start | bytes 3076
  51.5 17.5 %copy-start.8 = (bf16[8,2,12288]{2,1,0:T(2,128)(2,1)}, bf16[8,2,12288]{2,1,0:T(2,128)(2,1)S(1)}, u32[]{:S(2)}) copy-start(bf16[8,2,12288]{2,1,0:T(2,128)(2,1)S(1)} %all-to-all-done.2) | copy-start | bytes 1179652
  51.5 45.4 %all-to-all-start = ((bf16[8,2,36864]{2,1,0:T(2,128)(2,1)}), bf16[8,2,36864]{2,1,0:T(2,128)(2,1)}, u32[]{:S(2)}, u32[]{:S(2)}) async-start(bf16[8,2,36864]{2,1,0:T(2,128)(2,1)} %reshape.158), calls=%async_computation | async-start | bytes 2359296 | tf_op jit(solution)/shard_map/all_to_all | solution.py:89
  113.6 7.1 %copy-start.5 = (bf16[8,128,1,3,64]{4,0,3,1,2:T(8,128)(2,1)}, bf16[8,128,1,3,64]{4,0,3,1,2:T(8,128)(2,1)S(1)}, u32[]{:S(2)}) copy-start(bf16[8,128,1,3,64]{4,0,3,1,2:T(8,128)(2,1)S(1)} %copy.138) | copy-start | bytes 1179652
  120.7 1.5 copy-start.2
  120.7 1.7 copy-start.11
  122.4 3.9 %copy-start.9 = (bf16[24,8,8,128]{3,2,1,0:T(8,128)(2,1)S(1)}, bf16[24,8,8,128]{3,2,1,0:T(8,128)(2,1)}, u32[]{:S(2)}) copy-start(bf16[24,8,8,128]{3,2,1,0:T(8,128)(2,1)} %copy.143) | copy-start | bytes 1179652
  128.4 19.5 %all-to-all-start.1 = ((bf16[8,128,192]{1,2,0:T(8,128)(2,1)}), bf16[8,128,192]{1,2,0:T(8,128)(2,1)S(1)}, u32[]{:S(2)}, u32[]{:S(2)}) async-start(bf16[8,128,192]{1,2,0:T(8,128)(2,1)} %bitcast.149), calls=%async_computation.1 | async-start | bytes 786432 | tf_op jit(solution)/shard_map/all_to_all | solution.py:95
  134.1 3.8 %copy-start.3 = (f32[128,3,8,8]{2,3,1,0:T(8,128)S(1)}, f32[128,3,8,8]{2,3,1,0:T(8,128)}, u32[]{:S(2)}) copy-start(f32[128,3,8,8]{2,3,1,0:T(8,128)} %copy-done.2) | copy-start | bytes 294916
  137.9 1.1 copy-start.7
  139.0 1.1 copy-start.6
  140.2 1.1 copy-start.12
  147.9 37.7 %all-to-all-start.3 = ((bf16[8,128,576]{1,2,0:T(8,128)(2,1)}), bf16[8,128,576]{1,2,0:T(8,128)(2,1)}, u32[]{:S(2)}, u32[]{:S(2)}) async-start(bf16[8,128,576]{1,2,0:T(8,128)(2,1)} %bitcast.144), calls=%async_computation.3 | async-start | bytes 2359296 | tf_op jit(solution)/shard_map/all_to_all | solution.py:112
  153.9 72.9 %reduce-scatter.12.cloned.1.call-start = ((), (), s32[]{:S(2)}) async-start(), calls=%async_computation.10 | async-start | bytes 884736
  157.0 75.0 %all-reduce.5.cloned.1.call-start = ((), (), s32[]{:S(2)}) async-start(), calls=%async_computation.7 | async-start | bytes 3145728 | tf_op jit(solution)/shard_map/psum | solution.py:115
  189.5 1.0 copy-start.10
  189.5 70.8 %reduce-scatter.10.cloned.1.call-start = ((), (), s32[]{:S(2)}) async-start(), calls=%async_computation.9 | async-start | bytes 1966080
  204.4 125.2 %reduce-scatter.8.cloned.1.call-start = ((), (), s32[]{:S(2)}) async-start(), calls=%async_computation.8 | async-start | bytes 2654208 | tf_op jit(solution)/shard_map/reduce_scatter | solution.py:128
  232.0 2.0 copy-start.4
Sparse Core Ops, SparseCore 0:
  158.0 68.7 reduce-scatter.11
  229.4 27.0 reduce-scatter.9
  260.0 69.6 reduce-scatter.7
Sparse Core Ops, SparseCore 1:
  189.6 42.3 all-reduce.4
where the time goes:
time: 345 us; the launch traced here: 339 us
  waiting for transfers between devices  134 us (39%)
  local copies, waits for them, and re-layouts  72.4 us (21%)
  starting transfers between devices  34.6 us (10%)
  other arithmetic  34.4 us (10%)
  matrix products  25.9 us (8%)
  blocking collectives  21.8 us (6%)
  between operations  15.8 us (5%)
    reduce_scatter x1, waiting for transfers between devices, body(): lax.psum_scatter(qkv_part.reshape(row_width, 3, channels), 'tm', scatter_...  64.1 us
    unnamed x47, local copies, waits for them, and re-layouts  46.5 us
    all_to_all x1, waiting for transfers between devices, body(): lax.all_to_all(packed_cot_places, 'tm', split_axis=0, concat_axis=1, tile...  28.6 us
    all_to_all x1, waiting for transfers between devices, body(): lax.all_to_all(packed, 'tm', split_axis=1, concat_axis=0, tiled=True)  22 us
    psum x1, blocking collectives, body(): grad_gain = lax.psum(gain_part, 'tm')  21.8 us
    all_to_all x1, starting transfers between devices, body(): lax.all_to_all(packed, 'tm', split_axis=1, concat_axis=0, tiled=True)  17.1 us
    unnamed x2, other arithmetic  16 us
    unnamed x6, waiting for transfers between devices  15.5 us
  transfers between devices with their start and end apart: 8, of which 5 were waited for; matrix products, arithmetic and copies ran while one was open for 26% of the time, Pallas kernels for 0%

commit v1 on v0

v1 whole, which is shorter than its diff:
```python
import functools

import jax
import jax.numpy as jnp
from jax import lax
from jax.experimental import pallas as pl
from jax.experimental.pallas import tpu as pltpu
from jax.sharding import PartitionSpec as P

D = 768
H = 12
HEAD = D // H
LANES = 128
EPS = 1e-05
MASKED = -1000000000.0

BF = jnp.bfloat16
F32 = jnp.float32
VMEM_LIMIT = 16 * 1024 * 1024


def exchange(value, axis, bit):
    size = lax.axis_size(axis)
    return lax.ppermute(value, axis, [(i, i ^ bit) for i in range(size)])


def dot(a, b):
    return lax.dot_general(a, b, (((1,), (0,)), ((), ())), preferred_element_type=F32)


def dot_t(a, b):
    return lax.dot_general(a, b, (((1,), (1,)), ((), ())), preferred_element_type=F32)


def t_dot(a, b):
    return lax.dot_general(a, b, (((0,), (0,)), ((), ())), preferred_element_type=F32)


def standardize(x):
    x = x.astype(F32)
    shifted = x - jnp.mean(x, axis=-1, keepdims=True)
    inverse = lax.rsqrt(jnp.mean(shifted * shifted, axis=-1, keepdims=True) + EPS)
    return shifted * inverse, inverse


def block_rows(value, frames, b, rows):
    q = value.shape[0] // frames
    if q == rows:
        return value
    cut = value.reshape(frames, q, value.shape[1])[:, b * rows : (b + 1) * rows]
    return cut.reshape(frames * rows, value.shape[1])


def split_heads(value):
    lane = lax.broadcasted_iota(jnp.int32, value.shape, 1)
    zero = jnp.zeros_like(value)
    return jnp.concatenate(
        [jnp.where(lane < HEAD, value, zero), jnp.where(lane >= HEAD, value, zero)], axis=0
    )


def join_heads(value):
    n = value.shape[0] // 2
    lane = lax.broadcasted_iota(jnp.int32, (n, value.shape[1]), 1)
    return jnp.where(lane < HEAD, value[:n], value[n:])


def put_rows(ref, b, rows, col, value):
    ref[:, b * rows : (b + 1) * rows, col : col + value.shape[1]] = value.reshape(
        ref.shape[0], rows, value.shape[1]
    )


def all_rows(parts):
    return jnp.concatenate(list(parts), axis=0)


def halves(value, who):
    half = value.shape[-1] // 2
    low, high = value[..., :half], value[..., half:]
    first = who[0] // 2 == 0
    return jnp.where(first, low, high), jnp.where(first, high, low)


def own_and_other(value, who):
    share = value.shape[-1] // 2
    low, high = value[..., :share], value[..., share:]
    first = who[0] % 2 == 0
    return jnp.where(first, low, high), jnp.where(first, high, low)


def two_parts(value):
    top = value.astype(BF).astype(F32)
    return top, value - top


def send_kernel(n_near, n_slots, k, j, source, *refs):
    outs, sems = refs[:n_slots], refs[n_slots]
    copies = []
    for s in range(n_slots):
        if s < n_near:
            for g in range(2):
                copies.append((source.at[k[0] ^ s, j[0] ^ (2 * g)], outs[s].at[g]))
        else:
            copies.append((source.at[k[0] ^ s, j[0]], outs[s]))
    started = [
        pltpu.make_async_copy(src, dst, sems.at[i]) for i, (src, dst) in enumerate(copies)
    ]
    for copy in started:
        copy.start()
    for copy in started:
        copy.wait()


def attend_kernel(
    frames, rows, picks, who, where, gain, wa, wb, oa, ob, mask, x_in, *refs
):
    c_in = refs[: len(picks)]
    c_all, normed, mixed, pcot, keep, send, stats, gains = refs[len(picks) :]
    for s, (ref, pick) in enumerate(zip(c_in, picks)):
        if len(picks) == 1:
            c_all[...] = ref[...]
        else:
            c_all[where[0] ^ s] = ref[...] if pick is None else ref[pick]
    wq, wk, wv = (all_rows((wa[i], wb[i])) for i in range(3))
    wout = all_rows((oa[...], ob[...]))
    width, full = wout.shape
    chunk = x_in.shape[1]
    tokens = frames * chunk
    n_rows = frames * rows
    standard, _ = standardize(x_in[...].reshape(tokens, full))
    n = (standard * gain[...]).astype(BF)
    normed[...] = n
    qs, ks, vs = (dot_t(n, w).astype(BF) for w in (wq, wk, wv))
    c = c_all[...].reshape(tokens, full)
    mc = dot_t(c, wout).astype(BF)
    for b in range(chunk // rows):
        inside = mask[b]
        for p in range(width // LANES):
            cols = slice(p * LANES, (p + 1) * LANES)
            q, k, v, dm = (block_rows(z[:, cols], frames, b, rows) for z in (qs, ks, vs, mc))
            kk, vv = split_heads(k), split_heads(v)
            s = dot_t(q, kk) * HEAD ** (-0.5)
            dw = dot_t(dm, vv).astype(BF).astype(F32)
            w_parts, d_parts = [], []
            for e in range(2):
                part = jnp.where(inside > 0, s[:, e * n_rows : (e + 1) * n_rows], MASKED)
                top = jnp.max(part, axis=-1, keepdims=True)
                ex = jnp.exp(part - top) * inside
                total = jnp.sum(ex, axis=-1, keepdims=True)
                we = ex / jnp.where(total > 0, total, 1.0)
                de = dw[:, e * n_rows : (e + 1) * n_rows]
                inner = jnp.sum(we * de, axis=-1, keepdims=True)
                w_parts.append(we.astype(BF))
                d_parts.append((we * (de - inner) * HEAD ** (-0.5)).astype(BF))
            w = jnp.concatenate(w_parts, axis=1)
            ds = jnp.concatenate(d_parts, axis=1)
            put_rows(mixed, b, rows, p * LANES, dot(w, vv).astype(BF))
            put_rows(pcot, b, rows, p * LANES, dot(ds, kk).astype(BF))
            put_rows(pcot, b, rows, width + p * LANES, join_heads(t_dot(ds, q)).astype(BF))
            put_rows(pcot, b, rows, 2 * width + p * LANES, join_heads(t_dot(w, dm)).astype(BF))
    y = dot(mixed[...].reshape(tokens, width), wout)
    mine, other = halves(y, who)
    keep[0] = mine
    send[0] = other.astype(BF)
    pc = pcot[...].reshape(tokens, 3 * width)
    nc = dot(pc, all_rows((wq, wk, wv)))
    nn = n.astype(F32) * nc
    mean_plain = jnp.sum(nc * gain[...], axis=-1, keepdims=True)
    mean_cross = jnp.sum(nn, axis=-1, keepdims=True)
    total_gain = jnp.sum(nn, axis=0, keepdims=True) / gain[...]
    lane = lax.broadcasted_iota(jnp.int32, (tokens, LANES), 1)
    both = jnp.where(lane == 0, mean_plain, mean_cross) * (1.0 / full)
    half = full // 2
    stats[:, :tokens] = both.T[:8]
    mine, other = halves(nc, who)
    keep[1] = mine
    send[1] = other.astype(BF)
    mine, other = halves(total_gain, who)
    gains[...] = mine
    stats[:1, tokens : tokens + half] = other


def grads_kernel(n0, n1, p0, p1, c0, c1, m0, m1, keep, send):
    width = m0.shape[1]
    share = width // 2
    columns = []
    for which in range(3):
        cols = slice(which * width, (which + 1) * width)
        columns.append(t_dot(n0[...], p0[:, cols]) + t_dot(n1[...], p1[:, cols]))
    columns.append(t_dot(c0[...], m0[...]) + t_dot(c1[...], m1[...]))
    keep[...] = jnp.concatenate([v[:, :share] for v in columns], axis=1)
    send[...] = jnp.concatenate([v[:, share:] for v in columns], axis=1).astype(BF)


def halve_kernel(n_blocks, orders, step, n_held, where, *refs):
    held, moved, outs = refs[:n_held], refs[n_held : 2 * n_held], refs[2 * n_held :]
    k = where[0]
    for i, order in enumerate(orders):
        column = outs[2 * i].shape[-1]
        cols = slice(i * column, (i + 1) * column) if n_held == 1 else slice(None)
        keep, send = outs[2 * i : 2 * i + 2]
        source, came = held[i % n_held], moved[i % n_held]
        left = [bit for bit in (1 << b for b in range(n_blocks.bit_length())) if bit < n_blocks]
        left = [bit for bit in left if bit not in order[:step]]
        here = left.index(order[step])
        mine = (k // order[step]) % 2
        for n in range(keep.shape[0]):
            low = n % (1 << here)
            base = ((n >> here) << (here + 1)) + low
            stay = base + (mine << here)
            leave = base + ((1 - mine) << here)
            keep[n] = source[stay, :, cols] + came[stay, :, cols].astype(F32)
            send[n] = (source[leave, :, cols] + came[leave, :, cols].astype(F32)).astype(BF)


def last_grads_kernel(held_a, held_b, moved_a, moved_b, qkv, proj):
    share = proj.shape[0]
    a = held_a[0] + moved_a[0].astype(F32)
    b = held_b[0] + moved_b[0].astype(F32)
    qkv[0] = a[:, :share].astype(BF)
    qkv[1] = a[:, share:].astype(BF)
    qkv[2] = b[:, :share].astype(BF)
    proj[...] = b[:, share:].T.astype(BF)


def finish_kernel(who, x_in, c_in, gain, keep, recv, stats, stats_in, *refs):
    tokens = keep.shape[1]
    full = x_in.shape[-1]
    own, swap = refs[-2:] if len(refs) == 2 else refs[3:5]
    x = x_in[...].reshape(tokens, full)
    standard, inverse = standardize(x)
    both = (stats[:, :tokens] + stats_in[:, :tokens]).T
    mean_plain, mean_cross = both[:, 0:1], both[:, 1:2]
    out = halves(x.astype(F32), who)[0] + keep[0] + recv[0].astype(F32)
    scaled = (keep[1] + recv[1].astype(F32)) * halves(gain[...], who)[0]
    through = inverse * (scaled - mean_plain - halves(standard, who)[0] * mean_cross)
    back = halves(c_in[...].reshape(tokens, full).astype(F32), who)[0] + through
    for i, value in enumerate((out, back)):
        a, b = own_and_other(value, who)
        own[i] = a.astype(BF)
        swap[i * tokens : (i + 1) * tokens] = b.astype(BF)
    if len(refs) > 2:
        gains_a, gains_b, stats_other = refs[:3]
        own_gain = refs[5]
        half = full // 2
        sent = stats_in[:1, tokens : tokens + half] + stats_other[:1, tokens : tokens + half]
        a, b = own_and_other(gains_a[...] + gains_b[...] + sent, who)
        own_gain[...] = a
        top, rest = two_parts(b)
        row = lax.broadcasted_iota(jnp.int32, (16, b.shape[1]), 0)
        swap[2 * tokens :] = jnp.where(row == 0, top, jnp.where(row == 1, rest, 0.0)).astype(BF)


def pack_kernel(frames, who, own_a, own_b, recv_a, recv_b, own_gain, out, held):
    tokens, share = own_a.shape[1:]
    chunk = tokens // frames
    j = who[0]
    top = recv_a[2 * tokens : 2 * tokens + 2].astype(F32)
    value = own_gain[...] + top[:1] + top[1:]
    lanes = out.shape[2]
    n_parts = -(-share // lanes)
    extra = out.shape[1] - 2 * share
    block = jnp.zeros((extra, lanes), F32)
    at = lax.broadcasted_iota(jnp.int32, (extra, lanes), 0)
    row = 0
    for part in two_parts(value):
        if n_parts * lanes > share:
            part = jnp.concatenate([part, jnp.zeros((1, n_parts * lanes - share), F32)], axis=1)
        for i in range(n_parts):
            block = jnp.where(at == row, part[:, i * lanes : (i + 1) * lanes], block)
            row += 1
    for i in range(2):
        for s in range(frames):
            rows = slice(s * chunk, (s + 1) * chunk)
            sent = slice(i * tokens + s * chunk, i * tokens + (s + 1) * chunk)
            held[i, s, j] = own_a[i, rows].astype(F32)
            held[i, s, j ^ 2] = own_b[i, rows].astype(F32)
            held[i, s, j ^ 1] = recv_a[sent].astype(F32)
            held[i, s, j ^ 3] = recv_b[sent].astype(F32)
            turned = held[i, s].reshape(4 * chunk, share).T.astype(BF)
            out[s, i * share : (i + 1) * share] = turned
    for s in range(frames):
        out[s, 2 * share :] = block.astype(BF)


def assemble_kernel(parts, first, second, total, held, sems):
    n_slots, rows, lanes = parts.shape
    share = first.shape[0]
    copies = []
    for i, out in enumerate((first, second)):
        for s in range(n_slots):
            copies.append(
                pltpu.make_async_copy(
                    parts.at[s, pl.ds(i * share, share)],
                    out.at[:, pl.ds(s * lanes, lanes)],
                    sems.at[i * n_slots + s],
                )
            )
    copies.append(
        pltpu.make_async_copy(
            parts.at[:, pl.ds(2 * share, rows - 2 * share)], held, sems.at[2 * n_slots]
        )
    )
    for copy in copies:
        copy.start()
    for copy in copies:
        copy.wait()
    value = held[0].astype(F32)
    for s in range(1, n_slots):
        value = value + held[s].astype(F32)
    total[...] = value


def call(kernel, outs, *args, scalars=1, scratch=(), in_hbm=(), out_hbm=()):
    def space(i, hbm):
        return pl.BlockSpec(memory_space=pl.ANY if i in hbm else pltpu.VMEM)

    return pl.pallas_call(
        kernel,
        out_shape=[jax.ShapeDtypeStruct(shape, kind) for shape, kind in outs],
        in_specs=[pl.BlockSpec(memory_space=pltpu.SMEM)] * scalars
        + [space(i, in_hbm) for i in range(scalars, len(args))],
        out_specs=[space(i, out_hbm) for i in range(len(outs))],
        scratch_shapes=scratch,
        compiler_params=pltpu.CompilerParams(vmem_limit_bytes=VMEM_LIMIT),
    )(*args)


def block(frames_in, norm_gain, w_qkv, w_out, keep_runs, out_cotangent):
    _, place_total, width = frames_in.shape
    n_tm, n_te = lax.axis_size("tm"), lax.axis_size("tensor")
    frames = n_tm
    direct = n_tm <= 8
    n_near = n_tm // 2
    chunk = place_total // (n_tm * n_te)
    tokens = frames * chunk
    rows = 16 if chunk % 16 == 0 else chunk
    k = lax.axis_index("tm").astype(jnp.int32)
    j = lax.axis_index("tensor").astype(jnp.int32)
    where, who = k.reshape(1), j.reshape(1)
    share = w_qkv.shape[2]
    pair = 2 * share
    half = width // 2
    lanes = n_te * chunk

    w_own = jnp.transpose(w_qkv, (1, 2, 0))
    matrices = (w_own, exchange(w_own, "tensor", 1), w_out, exchange(w_out, "tensor", 1))
    gain = norm_gain.reshape(1, width)

    def gather_chunks(value):
        mine = lax.dynamic_index_in_dim(
            value.reshape(n_tm, n_te, chunk, width), j, 1, keepdims=False
        )
        first = lax.all_to_all(mine, "tm", split_axis=0, concat_axis=0, tiled=True)
        return first, exchange(first, "tensor", 2)

    xs = gather_chunks(frames_in)
    if direct:
        parts = call(
            functools.partial(send_kernel, n_near, n_tm),
            [((2, chunk, width), BF)] * n_near + [((chunk, width), BF)] * (n_tm - n_near),
            where, who, out_cotangent.reshape(n_tm, n_te, chunk, width),
            scalars=2, in_hbm=(2,), out_hbm=range(n_tm),
            scratch=[pltpu.SemaphoreType.DMA((n_tm + n_near,))],
        )
        far = [exchange(parts[s], "tm", s) for s in range(n_near, n_tm)]
        near = [parts[0]] + [exchange(parts[s], "tm", s) for s in range(1, n_near)]
        passed = [exchange(part, "tensor", 2) for part in far]
        cs = (near + far, near + passed)
        picks = [[g] * n_near + [None] * (n_tm - n_near) for g in range(2)]
    else:
        cs = tuple([value] for value in gather_chunks(out_cotangent))
        picks = [[None], [None]]

    starts = keep_runs[:, :, 0]
    ends = starts + keep_runs[:, :, 1]
    chunks = jnp.stack([j, j ^ 2])
    places = (
        k * (n_te * chunk) + chunks[:, None] * chunk + jnp.arange(chunk, dtype=jnp.int32)[None, :]
    )
    kept = jnp.any(
        (places[:, None, None, :] >= starts[None, :, :, None])
        & (places[:, None, None, :] < ends[None, :, :, None]),
        axis=2,
    )
    kept = kept.reshape(2, frames, chunk // rows, rows).transpose(0, 2, 1, 3)
    kept = kept.reshape(2, chunk // rows, frames * rows)
    place_of = jnp.arange(frames * rows, dtype=jnp.int32) % rows
    mask = (
        kept[:, :, :, None] & kept[:, :, None, :] & (place_of[:, None] == place_of[None, :])
    ).astype(F32)

    cube = (frames, chunk)
    done, recvs, stats_in = [], [], []
    for g in range(2):
        done.append(
            call(
                functools.partial(attend_kernel, frames, rows, picks[g]),
                [
                    (cube + (width,), BF),
                    ((tokens, width), BF),
                    (cube + (pair,), BF),
                    (cube + (3 * pair,), BF),
                    ((2, tokens, half), F32),
                    ((2, tokens, half), BF),
                    ((8, tokens + -(-half // LANES) * LANES), F32),
                    ((1, half), F32),
                ],
                who, where, gain, *matrices, mask[g], xs[g], *cs[g],
                scalars=2,
            )
        )
        recvs.append(exchange(done[g][5], "tensor", 2))
        stats_in.append(exchange(done[g][6], "tensor", 2))

    flat = lambda value: value.reshape(tokens, value.shape[-1])
    grad_keep, grad_send = call(
        grads_kernel,
        [((width, 4 * share), F32), ((width, 4 * share), BF)],
        done[0][1], done[1][1], flat(done[0][3]), flat(done[1][3]),
        flat(done[0][0]), flat(done[1][0]), flat(done[0][2]), flat(done[1][2]),
        scalars=0,
    )
    grad_recv = exchange(grad_send, "tensor", 1)
    per = width // n_tm
    bits = [1 << i for i in range(n_tm.bit_length() - 1)]
    column = 2 * share
    orders = (bits, bits[1::-1] + bits[2:])
    held = [grad_keep.reshape(n_tm, per, 4 * share)]
    moved = [grad_recv.reshape(n_tm, per, 4 * share)]
    for step in range(len(bits)):
        count = n_tm >> (step + 1)
        piece = (count, per, column)
        result = call(
            functools.partial(halve_kernel, n_tm, orders, step, len(held)),
            [(piece, F32), (piece, BF)] * 2,
            where, *held, *moved,
        )
        held = [result[0], result[2]]
        moved = [exchange(result[2 * i + 1], "tm", orders[i][step]) for i in range(2)]
    grad_qkv, grad_proj = call(
        last_grads_kernel,
        [((3, per, share), BF), ((share, per), BF)],
        *held, *moved,
        scalars=0,
    )
    grad_qkv = jnp.transpose(grad_qkv, (1, 0, 2))

    owns, swapped = [None, None], [None, None]
    for g in (1, 0):
        c_all, _, _, _, keep, _, stats, gains = done[g]
        outs = [((2, tokens, share), BF), ((2 * tokens + (0 if g else 16), share), BF)]
        more = ()
        if g == 0:
            outs.append(((1, share), F32))
            more = (gains, done[1][7], stats_in[0])
        result = call(
            finish_kernel, outs,
            who, xs[g], c_all, gain, keep, recvs[1 - g], stats, stats_in[1 - g], *more,
        )
        owns[g], swap = result[:2]
        swapped[g] = exchange(swap, "tensor", 1)
        if g == 0:
            own_gain = result[2]

    if direct:
        n_parts = -(-share // lanes)
        extra = -(-2 * n_parts // 16) * 16
        (message,) = call(
            functools.partial(pack_kernel, frames),
            [((frames, 2 * share + extra, lanes), BF)],
            who, *owns, *swapped, own_gain,
            scratch=[pltpu.VMEM((2, frames, n_te, chunk, share), F32)],
        )
        message = lax.all_to_all(message, "tm", split_axis=0, concat_axis=0, tiled=True)
        whole = ((share, place_total), BF)
        block_out, grad_in, total = call(
            assemble_kernel, [whole, whole, ((extra, lanes), F32)], message,
            scalars=0, in_hbm=(0,), out_hbm=(0, 1),
            scratch=[
                pltpu.VMEM((n_tm, extra, lanes), BF),
                pltpu.SemaphoreType.DMA((2 * n_tm + 1,)),
            ],
        )
        block_out, grad_in = block_out.T, grad_in.T
        grad_gain = (total[:n_parts] + total[n_parts : 2 * n_parts]).reshape(-1)[:share]
    else:
        order = jnp.arange(n_te, dtype=jnp.int32) ^ j
        four = jnp.stack(
            [owns[0], swapped[0][: 2 * tokens].reshape(2, tokens, share),
             owns[1], swapped[1].reshape(2, tokens, share)]
        )[order].reshape(n_te, 2, frames, chunk, share)
        message = jnp.transpose(four, (2, 1, 0, 3, 4)).reshape(frames, 2, lanes, share)
        message = lax.all_to_all(message, "tm", split_axis=0, concat_axis=0, tiled=True)
        block_out = message[:, 0].reshape(place_total, share)
        grad_in = message[:, 1].reshape(place_total, share)
        sent = swapped[0][2 * tokens : 2 * tokens + 2].astype(F32)
        grad_gain = lax.psum(own_gain[0] + sent[0] + sent[1], "tm")
    return (block_out[None], grad_in[None], grad_qkv, grad_proj, grad_gain)


def solution(mesh):
    in_specs = (
        P("tm", None, None),
        P(),
        P(None, None, "tensor"),
        P("tensor", None),
        P(),
        P("tm", None, None),
    )
    out_specs = (
        P("tm", None, "tensor"),
        P("tm", None, "tensor"),
        P("tm", None, "tensor"),
        P("tensor", "tm"),
        P("tensor"),
    )
    return jax.shard_map(block, mesh=mesh, in_specs=in_specs, out_specs=out_specs, check_vma=False)
```

time: 345 us -> 132 us (0.38); the launches traced: 339 us -> 131 us
  waiting for transfers between devices: 134 us -> 45.9 us
  local copies, waits for them, and re-layouts: 72.4 us -> 13.4 us
  other arithmetic: 34.4 us -> 5 us
  matrix products: 25.9 us -> 0 us
  Pallas kernels: 0 us -> 24.6 us
  blocking collectives: 21.8 us -> 0 us
  between operations: 15.8 us -> 0.82 us
  starting transfers between devices: 34.6 us -> 41.1 us
    reduce_scatter x1 -> x0, waiting for transfers between devices: 64.1 us -> none  [body(): lax.psum_scatter(qkv_part.reshape(row_width, 3, channels), 'tm', scatter_...]
    all_to_all x4 -> x2, waiting for transfers between devices: 50.6 us -> 0.01 us  [the longest x1 0.01 us: gather_chunks(): first = lax.all_to_all(mine, 'tm', split_axis=0, concat_axis=0, tiled=True)]
    ppermute x0 -> x27, waiting for transfers between devices: none -> 45.9 us  [exchange(): return lax.ppermute(value, axis, [(i, i ^ bit) for i in range(size)])]
    unnamed x47 -> x22, local copies, waits for them, and re-layouts: 46.5 us -> 7.31 us
    ppermute x0 -> x27, starting transfers between devices: none -> 29.6 us  [exchange(): return lax.ppermute(value, axis, [(i, i ^ bit) for i in range(size)])]
    pallas_call x0 -> x12, Pallas kernels: none -> 24.6 us  [call(): pl.pallas_call(kernel, out_shape=[jax.ShapeDtypeStruct(shape, kind) for s...]
    dot_general x11 -> x0, matrix products: 22.9 us -> none  [the longest x2 6.05 us: back_project(): lax.dot_general(cotangent.reshape(-1, cotangent.shape[-1]), weight, (((1,...]
    all_to_all x4 -> x2, starting transfers between devices: 34.3 us -> 11.5 us  [the longest x1 7.31 us: gather_chunks(): first = lax.all_to_all(mine, 'tm', split_axis=0, concat_axis=0, tiled=True)]
  transfers between devices with their start and end apart: 8 -> 29, of which waited for: 5 -> 14; matrix products, arithmetic and copies ran while one was open for 26% -> 7% of each run, Pallas kernels for 0% -> 13%
where the time goes in v1:
time: 132 us; the launch traced here: 131 us
  waiting for transfers between devices  45.9 us (35%)
  starting transfers between devices  41.1 us (31%)
  Pallas kernels  24.6 us (19%)
  local copies, waits for them, and re-layouts  13.4 us (10%)
  other arithmetic  5 us (4%)
    ppermute x27, waiting for transfers between devices, exchange(): return lax.ppermute(value, axis, [(i, i ^ bit) for i in range(size)])  45.9 us
    ppermute x27, starting transfers between devices, exchange(): return lax.ppermute(value, axis, [(i, i ^ bit) for i in range(size)])  29.6 us
    pallas_call x12, Pallas kernels, call(): pl.pallas_call(kernel, out_shape=[jax.ShapeDtypeStruct(shape, kind) for s...  24.6 us
    all_to_all x1, starting transfers between devices, gather_chunks(): first = lax.all_to_all(mine, 'tm', split_axis=0, concat_axis=0, tiled=True)  7.31 us
    unnamed x22, local copies, waits for them, and re-layouts  7.31 us
    all_to_all x1, starting transfers between devices, block(): lax.all_to_all(message, 'tm', split_axis=0, concat_axis=0, tiled=True)  4.18 us
  transfers between devices with their start and end apart: 29, of which 14 were waited for; matrix products, arithmetic and copies ran while one was open for 7% of the time, Pallas kernels for 13%

profile of v1, /device:TPU:0, one launch (start us, length us, event | category | flops | bytes accessed | tf_op | source)
XLA Modules:
  0.0 130.8 jit_solution(10608535827046149757)
XLA Ops:
  2.8 7.3 %all-to-all-start = ((bf16[8,32,768]{2,1,0:T(8,128)(2,1)}), bf16[8,32,768]{2,1,0:T(8,128)(2,1)}, u32[]{:S(2)}, u32[]{:S(2)}) async-start(bf16[8,32,768]{2,1,0:T(8,128)(2,1)} %dynamic-slice_bitcast_fusion), calls=%async_computation | async-start | bytes 786432 | tf_op jit(solution)/shard_map/all_to_all | solution.py:355
  14.6 1.9 %collective-permute-start.2 = (bf16[2,32,768]{2,1,0:T(8,128)(2,1)}, bf16[2,32,768]{2,1,0:T(8,128)(2,1)S(1)}, u32[]{:S(2)}, u32[]{:S(2)}) collective-permute-start(bf16[2,32,768]{2,1,0:T(8,128)(2,1)} %get-tuple-element.54), channel_id=1, source_target_pairs={{0,4},{4,0},{8,12},{12,8},{16,20},{20,16},{24,28},{28,24},{1,5},{5... | collective-permute-start | bytes 294920 | tf_op jit(solution)/shard_map/ppermute | solution.py:24
  16.6 2.4 %collective-permute-start.5 = (bf16[32,768]{1,0:T(8,128)(2,1)}, bf16[32,768]{1,0:T(8,128)(2,1)}, u32[]{:S(2)}, u32[]{:S(2)}) collective-permute-start(bf16[32,768]{1,0:T(8,128)(2,1)} %get-tuple-element.57), channel_id=1, source_target_pairs={{0,16},{4,20},{8,24},{12,28},{16,0},{20,4},{24,8},{28,12},{1,17},{... | collective-permute-start | bytes 147464 | tf_op jit(solution)/shard_map/ppermute | solution.py:24
  19.0 3.7 %collective-permute-start.7 = (bf16[32,768]{1,0:T(8,128)(2,1)}, bf16[32,768]{1,0:T(8,128)(2,1)}, u32[]{:S(2)}, u32[]{:S(2)}) collective-permute-start(bf16[32,768]{1,0:T(8,128)(2,1)} %get-tuple-element.59), channel_id=1, source_target_pairs={{0,24},{4,28},{8,16},{12,20},{16,8},{20,12},{24,0},{28,4},{1,25},{... | collective-permute-start | bytes 147464 | tf_op jit(solution)/shard_map/ppermute | solution.py:24
  25.6 1.6 %collective-permute-done.5.refs_4_ = bf16[32,768]{1,0:T(8,128)(2,1)} collective-permute-done((bf16[32,768]{1,0:T(8,128)(2,1)}, bf16[32,768]{1,0:T(8,128)(2,1)}, u32[]{:S(2)}, u32[]{:S(2)}) %collective-permute-start.5) | collective-permute-done | bytes 49184 | tf_op jit(solution)/shard_map/ppermute | solution.py:24
  35.5 1.7 %collective-permute-done.8.refs_7_ = bf16[32,768]{1,0:T(8,128)(2,1)} collective-permute-done((bf16[32,768]{1,0:T(8,128)(2,1)}, bf16[32,768]{1,0:T(8,128)(2,1)}, u32[]{:S(2)}, u32[]{:S(2)}) %collective-permute-start.8) | collective-permute-done | bytes 49184 | tf_op jit(solution)/shard_map/ppermute | solution.py:24
  37.2 1.5 %collective-permute-start.10 = (bf16[32,768]{1,0:T(8,128)(2,1)}, bf16[32,768]{1,0:T(8,128)(2,1)}, u32[]{:S(2)}, u32[]{:S(2)}) collective-permute-start(bf16[32,768]{1,0:T(8,128)(2,1)} %collective-permute-done.5.refs_4_), channel_id=1, source_target_pairs={{0,2},{1,3},{2,0},{3,1},{4,6},{5,7},{6,4},{7,5},{8,10},{9,11},{10,... | collective-permute-start | bytes 147464 | tf_op jit(solution)/shard_map/ppermute | solution.py:24
  39.2 1.5 %collective-permute-start.9 = (bf16[8,32,768]{2,1,0:T(8,128)(2,1)}, bf16[8,32,768]{2,1,0:T(8,128)(2,1)S(1)}, u32[]{:S(2)}, u32[]{:S(2)}) collective-permute-start(bf16[8,32,768]{2,1,0:T(8,128)(2,1)} %all-to-all-done.x_in), channel_id=1, source_target_pairs={{0,2},{1,3},{2,0},{3,1},{4,6},{5,7},{6,4},{7,5},{8,10},{9,11},{10,... | collective-permute-start | bytes 1179656 | tf_op jit(solution)/shard_map/ppermute | solution.py:24
  41.6 2.0 %collective-permute-start.12 = (bf16[32,768]{1,0:T(8,128)(2,1)}, bf16[32,768]{1,0:T(8,128)(2,1)S(1)}, u32[]{:S(2)}, u32[]{:S(2)}) collective-permute-start(bf16[32,768]{1,0:T(8,128)(2,1)} %collective-permute-done.7.refs_6_), channel_id=1, source_target_pairs={{0,2},{1,3},{2,0},{3,1},{4,6},{5,7},{6,4},{7,5},{8,10},{9,11},{10,... | collective-permute-start | bytes 147464 | tf_op jit(solution)/shard_map/ppermute | solution.py:24
  45.4 7.4 %collective-permute-done.12.refs_6_ = bf16[32,768]{1,0:T(8,128)(2,1)S(1)} collective-permute-done((bf16[32,768]{1,0:T(8,128)(2,1)}, bf16[32,768]{1,0:T(8,128)(2,1)S(1)}, u32[]{:S(2)}, u32[]{:S(2)}) %collective-permute-start.12) | collective-permute-done | bytes 49184 | tf_op jit(solution)/shard_map/ppermute | solution.py:24
  54.3 6.4 %shard_map.103 = (bf16[8,32,768]{2,1,0:T(8,128)(2,1)S(1)}, bf16[256,768]{1,0:T(8,128)(2,1)S(1)}, bf16[8,32,384]{2,1,0:T(8,128)(2,1)S(1)}, bf16[8,32,1152]{2,1,0:...) custom-call(s32[1]{0:T(128)} %bitcast.j.who, ...), custom_call_target="tpu_custom_call" | custom-call | tf_op jit(solution)/shard_map/pallas_call | solution.py:319
  62.1 6.5 %shard_map.102 = (bf16[8,32,768]{2,1,0:T(8,128)(2,1)S(1)}, bf16[256,768]{1,0:T(8,128)(2,1)S(1)}, bf16[8,32,384]{2,1,0:T(8,128)(2,1)S(1)}, bf16[8,32,1152]{2,1,0:...) custom-call(s32[1]{0:T(128)} %bitcast.j.who, ...), custom_call_target="tpu_custom_call" | custom-call | tf_op jit(solution)/shard_map/pallas_call | solution.py:319
  69.2 2.9 %shard_map.108 = (f32[768,768]{1,0:T(8,128)S(1)}, bf16[768,768]{1,0:T(8,128)(2,1)}) custom-call(bf16[256,768]{1,0:T(8,128)(2,1)S(1)} %get-tuple-element.78.n0, bf16[256,768]{1,0:T(8,128)(2,1)S(1)} %get-tuple-element.79.n1, bf16[256,1152]{1,0:T(8,128)(2,1)S(1)} %bitcast.50, bf16[256,1152]{1,0:T(8,128)(2,1)S(1)} %bitcast.49, bf16[256,768]{1,0:T(8,128)(2,1)S(1)} %bitcast.48, ...), custom_call_target="tpu_custom_call" | custom-call | tf_op jit(solution)/shard_map/pallas_call | solution.py:319
  74.2 6.0 %collective-permute-done.16.refs_2_.stats_in = f32[8,640]{1,0:T(8,128)S(1)} collective-permute-done((f32[8,640]{1,0:T(8,128)S(1)}, f32[8,640]{1,0:T(8,128)S(1)}, u32[]{:S(2)}, u32[]{:S(2)}) %collective-permute-start.16) | collective-permute-done | bytes 20512 | tf_op jit(solution)/shard_map/ppermute | solution.py:24
  80.4 2.0 %shard_map.104 = (bf16[2,256,192]{2,1,0:T(8,128)(2,1)S(1)}, bf16[528,192]{1,0:T(8,128)(2,1)S(1)}, f32[1,192]{1,0:T(1,128)S(1)}) custom-call(s32[1]{0:T(128)} %bitcast.j.who, bf16[8,32,768]{2,1,0:T(8,128)(2,1)} %all-to-all-done.x_in, bf16[8,32,768]{2,1,0:T(8,128)(2,1)S(1)} %get-tuple-element.61.c_in, f32[1,768]{1,0:T(1,128)S(1)} %reshape.152.gain, ...), custom_call_target="tpu_custom_call" | custom-call | tf_op jit(solution)/shard_map/pallas_call | solution.py:319
  86.4 4.2 %all-to-all-start.1 = ((bf16[8,400,128]{2,1,0:T(8,128)(2,1)}), bf16[8,400,128]{2,1,0:T(8,128)(2,1)S(1)}, u32[]{:S(2)}, u32[]{:S(2)}) async-start(bf16[8,400,128]{2,1,0:T(8,128)(2,1)} %shard_map.106), calls=%async_computation.1 | async-start | bytes 1638400 | tf_op jit(solution)/shard_map/all_to_all | solution.py:476
  90.6 1.7 %copy-done.3 = f32[768,768]{1,0:T(8,128)S(1)} copy-done((f32[768,768]{1,0:T(8,128)S(1)}, f32[768,768]{1,0:T(8,128)}, u32[]{:S(2)}) %copy-start.3) | copy-done | bytes 2359320
  93.8 2.1 %collective-permute-start.21 = (bf16[4,96,384]{2,1,0:T(8,128)(2,1)S(1)}, bf16[4,96,384]{2,1,0:T(8,128)(2,1)S(1)}, u32[]{:S(2)}, u32[]{:S(2)}) collective-permute-start(bf16[4,96,384]{2,1,0:T(8,128)(2,1)S(1)} %get-tuple-element.88), channel_id=1, source_target_pairs={{0,4},{4,0},{8,12},{12,8},{16,20},{20,16},{24,28},{28,24},{1,5},{5... | collective-permute-start | bytes 884744 | tf_op jit(solution)/shard_map/ppermute | solution.py:24
  97.3 11.3 %collective-permute-done.21.refs_2_ = bf16[4,96,384]{2,1,0:T(8,128)(2,1)S(1)} collective-permute-done((bf16[4,96,384]{2,1,0:T(8,128)(2,1)S(1)}, bf16[4,96,384]{2,1,0:T(8,128)(2,1)S(1)}, u32[]{:S(2)}, u32[]{:S(2)}) %collective-permute-start.21) | collective-permute-done | bytes 294944 | tf_op jit(solution)/shard_map/ppermute | solution.py:24
  108.6 4.4 %collective-permute-done.22.refs_3_ = bf16[4,96,384]{2,1,0:T(8,128)(2,1)S(1)} collective-permute-done((bf16[4,96,384]{2,1,0:T(8,128)(2,1)S(1)}, bf16[4,96,384]{2,1,0:T(8,128)(2,1)S(1)}, u32[]{:S(2)}, u32[]{:S(2)}) %collective-permute-start.22) | collective-permute-done | bytes 294944 | tf_op jit(solution)/shard_map/ppermute | solution.py:24
  115.3 3.2 %collective-permute-done.23.refs_2_ = bf16[2,96,384]{2,1,0:T(8,128)(2,1)S(1)} collective-permute-done((bf16[2,96,384]{2,1,0:T(8,128)(2,1)S(1)}, bf16[2,96,384]{2,1,0:T(8,128)(2,1)S(1)}, u32[]{:S(2)}, u32[]{:S(2)}) %collective-permute-start.23) | collective-permute-done | bytes 147488 | tf_op jit(solution)/shard_map/ppermute | solution.py:24
  119.3 2.2 %collective-permute-start.25 = (bf16[1,96,384]{2,1,0:T(8,128)(2,1)S(1)}, bf16[1,96,384]{2,1,0:T(8,128)(2,1)S(1)}, u32[]{:S(2)}, u32[]{:S(2)}) collective-permute-start(bf16[1,96,384]{2,1,0:T(8,128)(2,1)S(1)} %get-tuple-element.96), channel_id=1, source_target_pairs={{0,16},{4,20},{8,24},{12,28},{16,0},{20,4},{24,8},{28,12},{1,17},{... | collective-permute-start | bytes 221192 | tf_op jit(solution)/shard_map/ppermute | solution.py:24
  122.3 4.5 %collective-permute-done.25.moved_a = bf16[1,96,384]{2,1,0:T(8,128)(2,1)S(1)} collective-permute-done((bf16[1,96,384]{2,1,0:T(8,128)(2,1)S(1)}, bf16[1,96,384]{2,1,0:T(8,128)(2,1)S(1)}, u32[]{:S(2)}, u32[]{:S(2)}) %collective-permute-start.25) | collective-permute-done | bytes 73760 | tf_op jit(solution)/shard_map/ppermute | solution.py:24
  126.8 1.6 %collective-permute-done.26.moved_b = bf16[1,96,384]{2,1,0:T(8,128)(2,1)S(1)} collective-permute-done((bf16[1,96,384]{2,1,0:T(8,128)(2,1)S(1)}, bf16[1,96,384]{2,1,0:T(8,128)(2,1)S(1)}, u32[]{:S(2)}, u32[]{:S(2)}) %collective-permute-start.26) | collective-permute-done | bytes 73760 | tf_op jit(solution)/shard_map/ppermute | solution.py:24
  (83 shorter events, 39.9 us)
Async XLA Ops:
  2.8 36.4 %all-to-all-start = ((bf16[8,32,768]{2,1,0:T(8,128)(2,1)}), bf16[8,32,768]{2,1,0:T(8,128)(2,1)}, u32[]{:S(2)}, u32[]{:S(2)}) async-start(bf16[8,32,768]{2,1,0:T(8,128)(2,1)} %dynamic-slice_bitcast_fusion), calls=%async_computation | async-start | bytes 786432 | tf_op jit(solution)/shard_map/all_to_all | solution.py:355
  10.1 43.2 %collective-permute-start = (bf16[3,192,768]{2,1,0:T(8,128)(2,1)S(1)}, bf16[3,192,768]{2,1,0:T(8,128)(2,1)S(1)}, u32[]{:S(2)}, u32[]{:S(2)}) collective-permute-start(bf16[3,192,768]{2,1,0:T(8,128)(2,1)S(1)} %bitcast.42), channel_id=1, source_target_pairs={{0,1},{1,0},{2,3},{3,2},{4,5},{5,4},{6,7},{7,6},{8,9},{9,8},{10,11... | collective-permute-start | bytes 2654216 | tf_op jit(solution)/shard_map/ppermute | solution.py:24
  14.6 22.5 %collective-permute-start.2 = (bf16[2,32,768]{2,1,0:T(8,128)(2,1)}, bf16[2,32,768]{2,1,0:T(8,128)(2,1)S(1)}, u32[]{:S(2)}, u32[]{:S(2)}) collective-permute-start(bf16[2,32,768]{2,1,0:T(8,128)(2,1)} %get-tuple-element.54), channel_id=1, source_target_pairs={{0,4},{4,0},{8,12},{12,8},{16,20},{20,16},{24,28},{28,24},{1,5},{5... | collective-permute-start | bytes 294920 | tf_op jit(solution)/shard_map/ppermute | solution.py:24
  16.6 10.6 %collective-permute-start.5 = (bf16[32,768]{1,0:T(8,128)(2,1)}, bf16[32,768]{1,0:T(8,128)(2,1)}, u32[]{:S(2)}, u32[]{:S(2)}) collective-permute-start(bf16[32,768]{1,0:T(8,128)(2,1)} %get-tuple-element.57), channel_id=1, source_target_pairs={{0,16},{4,20},{8,24},{12,28},{16,0},{20,4},{24,8},{28,12},{1,17},{... | collective-permute-start | bytes 147464 | tf_op jit(solution)/shard_map/ppermute | solution.py:24
  19.0 9.7 %collective-permute-start.6 = (bf16[32,768]{1,0:T(8,128)(2,1)}, bf16[32,768]{1,0:T(8,128)(2,1)}, u32[]{:S(2)}, u32[]{:S(2)}) collective-permute-start(bf16[32,768]{1,0:T(8,128)(2,1)} %get-tuple-element.58), channel_id=1, source_target_pairs={{0,20},{4,16},{8,28},{12,24},{16,4},{20,0},{24,12},{28,8},{1,21},{... | collective-permute-start | bytes 147464 | tf_op jit(solution)/shard_map/ppermute | solution.py:24
  19.0 11.0 %collective-permute-start.7 = (bf16[32,768]{1,0:T(8,128)(2,1)}, bf16[32,768]{1,0:T(8,128)(2,1)}, u32[]{:S(2)}, u32[]{:S(2)}) collective-permute-start(bf16[32,768]{1,0:T(8,128)(2,1)} %get-tuple-element.59), channel_id=1, source_target_pairs={{0,24},{4,28},{8,16},{12,20},{16,8},{20,12},{24,0},{28,4},{1,25},{... | collective-permute-start | bytes 147464 | tf_op jit(solution)/shard_map/ppermute | solution.py:24
  27.2 11.5 %collective-permute-start.3 = (bf16[2,32,768]{2,1,0:T(8,128)(2,1)}, bf16[2,32,768]{2,1,0:T(8,128)(2,1)}, u32[]{:S(2)}, u32[]{:S(2)}) collective-permute-start(bf16[2,32,768]{2,1,0:T(8,128)(2,1)} %copy-done.8), channel_id=1, source_target_pairs={{0,8},{4,12},{8,0},{12,4},{16,24},{20,28},{24,16},{28,20},{1,9},{5... | collective-permute-start | bytes 294920 | tf_op jit(solution)/shard_map/ppermute | solution.py:24
  28.6 10.6 %collective-permute-start.4 = (bf16[2,32,768]{2,1,0:T(8,128)(2,1)}, bf16[2,32,768]{2,1,0:T(8,128)(2,1)}, u32[]{:S(2)}, u32[]{:S(2)}) collective-permute-start(bf16[2,32,768]{2,1,0:T(8,128)(2,1)} %copy-done.7), channel_id=1, source_target_pairs={{0,12},{4,8},{8,4},{12,0},{16,28},{20,24},{24,20},{28,16},{1,13},{... | collective-permute-start | bytes 294920 | tf_op jit(solution)/shard_map/ppermute | solution.py:24
  30.1 7.1 %collective-permute-start.8 = (bf16[32,768]{1,0:T(8,128)(2,1)}, bf16[32,768]{1,0:T(8,128)(2,1)}, u32[]{:S(2)}, u32[]{:S(2)}) collective-permute-start(bf16[32,768]{1,0:T(8,128)(2,1)} %copy-done.9), channel_id=1, source_target_pairs={{0,28},{4,24},{8,20},{12,16},{16,12},{20,8},{24,4},{28,0},{1,29},{... | collective-permute-start | bytes 147464 | tf_op jit(solution)/shard_map/ppermute | solution.py:24
  37.2 16.1 %collective-permute-start.1 = (bf16[192,768]{1,0:T(8,128)(2,1)}, bf16[192,768]{1,0:T(8,128)(2,1)}, u32[]{:S(2)}, u32[]{:S(2)}) collective-permute-start(bf16[192,768]{1,0:T(8,128)(2,1)} %oa.3), channel_id=1, source_target_pairs={{0,1},{1,0},{2,3},{3,2},{4,5},{5,4},{6,7},{7,6},{8,9},{9,8},{10,11... | collective-permute-start | bytes 884744 | tf_op jit(solution)/shard_map/ppermute | solution.py:24
  39.2 14.1 %collective-permute-start.9 = (bf16[8,32,768]{2,1,0:T(8,128)(2,1)}, bf16[8,32,768]{2,1,0:T(8,128)(2,1)S(1)}, u32[]{:S(2)}, u32[]{:S(2)}) collective-permute-start(bf16[8,32,768]{2,1,0:T(8,128)(2,1)} %all-to-all-done.x_in), channel_id=1, source_target_pairs={{0,2},{1,3},{2,0},{3,1},{4,6},{5,7},{6,4},{7,5},{8,10},{9,11},{10,... | collective-permute-start | bytes 1179656 | tf_op jit(solution)/shard_map/ppermute | solution.py:24
  41.6 11.1 %collective-permute-start.12 = (bf16[32,768]{1,0:T(8,128)(2,1)}, bf16[32,768]{1,0:T(8,128)(2,1)S(1)}, u32[]{:S(2)}, u32[]{:S(2)}) collective-permute-start(bf16[32,768]{1,0:T(8,128)(2,1)} %collective-permute-done.7.refs_6_), channel_id=1, source_target_pairs={{0,2},{1,3},{2,0},{3,1},{4,6},{5,7},{6,4},{7,5},{8,10},{9,11},{10,... | collective-permute-start | bytes 147464 | tf_op jit(solution)/shard_map/ppermute | solution.py:24
  43.6 9.7 %collective-permute-start.13 = (bf16[32,768]{1,0:T(8,128)(2,1)}, bf16[32,768]{1,0:T(8,128)(2,1)S(1)}, u32[]{:S(2)}, u32[]{:S(2)}) collective-permute-start(bf16[32,768]{1,0:T(8,128)(2,1)} %collective-permute-done.8.refs_7_), channel_id=1, source_target_pairs={{0,2},{1,3},{2,0},{3,1},{4,6},{5,7},{6,4},{7,5},{8,10},{9,11},{10,... | collective-permute-start | bytes 147464 | tf_op jit(solution)/shard_map/ppermute | solution.py:24
  60.7 19.7 %collective-permute-start.14 = (bf16[2,256,384]{2,1,0:T(8,128)(2,1)S(1)}, bf16[2,256,384]{2,1,0:T(8,128)(2,1)S(1)}, u32[]{:S(2)}, u32[]{:S(2)}) collective-permute-start(bf16[2,256,384]{2,1,0:T(8,128)(2,1)S(1)} %get-tuple-element.63), channel_id=1, source_target_pairs={{0,2},{1,3},{2,0},{3,1},{4,6},{5,7},{6,4},{7,5},{8,10},{9,11},{10,... | collective-permute-start | bytes 1179656 | tf_op jit(solution)/shard_map/ppermute | solution.py:24
  68.5 14.0 %collective-permute-start.17 = (bf16[2,256,384]{2,1,0:T(8,128)(2,1)S(1)}, bf16[2,256,384]{2,1,0:T(8,128)(2,1)S(1)}, u32[]{:S(2)}, u32[]{:S(2)}) collective-permute-start(bf16[2,256,384]{2,1,0:T(8,128)(2,1)S(1)} %get-tuple-element.71), channel_id=1, source_target_pairs={{0,2},{1,3},{2,0},{3,1},{4,6},{5,7},{6,4},{7,5},{8,10},{9,11},{10,... | collective-permute-start | bytes 1179656 | tf_op jit(solution)/shard_map/ppermute | solution.py:24
  72.2 18.4 %collective-permute-start.20 = (bf16[768,768]{1,0:T(8,128)(2,1)}, bf16[768,768]{1,0:T(8,128)(2,1)}, u32[]{:S(2)}, u32[]{:S(2)}) collective-permute-start(bf16[768,768]{1,0:T(8,128)(2,1)} %get-tuple-element.85), channel_id=1, source_target_pairs={{0,1},{1,0},{2,3},{3,2},{4,5},{5,4},{6,7},{7,6},{8,9},{9,8},{10,11... | collective-permute-start | bytes 3538952 | tf_op jit(solution)/shard_map/ppermute | solution.py:24
  72.2 8.0 %collective-permute-start.16 = (f32[8,640]{1,0:T(8,128)S(1)}, f32[8,640]{1,0:T(8,128)S(1)}, u32[]{:S(2)}, u32[]{:S(2)}) collective-permute-start(f32[8,640]{1,0:T(8,128)S(1)} %get-tuple-element.64.stats), channel_id=1, source_target_pairs={{0,2},{1,3},{2,0},{3,1},{4,6},{5,7},{6,4},{7,5},{8,10},{9,11},{10,... | collective-permute-start | bytes 61448 | tf_op jit(solution)/shard_map/ppermute | solution.py:24
  73.5 6.9 %collective-permute-start.15 = (f32[8,640]{1,0:T(8,128)S(1)}, f32[8,640]{1,0:T(8,128)S(1)}, u32[]{:S(2)}, u32[]{:S(2)}) collective-permute-start(f32[8,640]{1,0:T(8,128)S(1)} %get-tuple-element.65.stats), channel_id=1, source_target_pairs={{0,2},{1,3},{2,0},{3,1},{4,6},{5,7},{6,4},{7,5},{8,10},{9,11},{10,... | collective-permute-start | bytes 61448 | tf_op jit(solution)/shard_map/ppermute | solution.py:24
  86.4 42.7 %all-to-all-start.1 = ((bf16[8,400,128]{2,1,0:T(8,128)(2,1)}), bf16[8,400,128]{2,1,0:T(8,128)(2,1)S(1)}, u32[]{:S(2)}, u32[]{:S(2)}) async-start(bf16[8,400,128]{2,1,0:T(8,128)(2,1)} %shard_map.106), calls=%async_computation.1 | async-start | bytes 1638400 | tf_op jit(solution)/shard_map/all_to_all | solution.py:476
  93.8 14.9 %collective-permute-start.21 = (bf16[4,96,384]{2,1,0:T(8,128)(2,1)S(1)}, bf16[4,96,384]{2,1,0:T(8,128)(2,1)S(1)}, u32[]{:S(2)}, u32[]{:S(2)}) collective-permute-start(bf16[4,96,384]{2,1,0:T(8,128)(2,1)S(1)} %get-tuple-element.88), channel_id=1, source_target_pairs={{0,4},{4,0},{8,12},{12,8},{16,20},{20,16},{24,28},{28,24},{1,5},{5... | collective-permute-start | bytes 884744 | tf_op jit(solution)/shard_map/ppermute | solution.py:24
  95.8 17.2 %collective-permute-start.22 = (bf16[4,96,384]{2,1,0:T(8,128)(2,1)S(1)}, bf16[4,96,384]{2,1,0:T(8,128)(2,1)S(1)}, u32[]{:S(2)}, u32[]{:S(2)}) collective-permute-start(bf16[4,96,384]{2,1,0:T(8,128)(2,1)S(1)} %get-tuple-element.89), channel_id=1, source_target_pairs={{0,8},{4,12},{8,0},{12,4},{16,24},{20,28},{24,16},{28,20},{1,9},{5... | collective-permute-start | bytes 884744 | tf_op jit(solution)/shard_map/ppermute | solution.py:24
  113.2 5.3 %collective-permute-start.23 = (bf16[2,96,384]{2,1,0:T(8,128)(2,1)S(1)}, bf16[2,96,384]{2,1,0:T(8,128)(2,1)S(1)}, u32[]{:S(2)}, u32[]{:S(2)}) collective-permute-start(bf16[2,96,384]{2,1,0:T(8,128)(2,1)S(1)} %get-tuple-element.92), channel_id=1, source_target_pairs={{0,8},{4,12},{8,0},{12,4},{16,24},{20,28},{24,16},{28,20},{1,9},{5... | collective-permute-start | bytes 442376 | tf_op jit(solution)/shard_map/ppermute | solution.py:24
  119.3 7.5 %collective-permute-start.25 = (bf16[1,96,384]{2,1,0:T(8,128)(2,1)S(1)}, bf16[1,96,384]{2,1,0:T(8,128)(2,1)S(1)}, u32[]{:S(2)}, u32[]{:S(2)}) collective-permute-start(bf16[1,96,384]{2,1,0:T(8,128)(2,1)S(1)} %get-tuple-element.96), channel_id=1, source_target_pairs={{0,16},{4,20},{8,24},{12,28},{16,0},{20,4},{24,8},{28,12},{1,17},{... | collective-permute-start | bytes 221192 | tf_op jit(solution)/shard_map/ppermute | solution.py:24
  121.5 6.8 %collective-permute-start.26 = (bf16[1,96,384]{2,1,0:T(8,128)(2,1)S(1)}, bf16[1,96,384]{2,1,0:T(8,128)(2,1)S(1)}, u32[]{:S(2)}, u32[]{:S(2)}) collective-permute-start(bf16[1,96,384]{2,1,0:T(8,128)(2,1)S(1)} %get-tuple-element.97), channel_id=1, source_target_pairs={{0,16},{4,20},{8,24},{12,28},{16,0},{20,4},{24,8},{28,12},{1,17},{... | collective-permute-start | bytes 221192 | tf_op jit(solution)/shard_map/ppermute | solution.py:24
  (16 other events, 75.4 us)

commit v2 on v1

--- a/solution.py
+++ b/solution.py
@@ -16,7 +16,8 @@
 
 BF = jnp.bfloat16
 F32 = jnp.float32
-VMEM_LIMIT = 16 * 1024 * 1024
+VMEM_LIMIT = 12 * 1024 * 1024
+WHOLE_VMEM = 61*1024*1024
 
 
 def exchange(value, axis, bit):
@@ -94,34 +95,60 @@
     return top, value - top
 
 
-def send_kernel(n_near, n_slots, k, j, source, *refs):
+def copy_all(pairs, sems):
+    copies = [pltpu.make_async_copy(src, dst, sems.at[i]) for i, (src, dst) in enumerate(pairs)]
+    for copy in copies:
+        copy.start()
+    for copy in copies:
+        copy.wait()
+
+
+def send_x_kernel(j, x_in, x_out, sems):
+    copy_all([(x_in.at[i, j[0]], x_out.at[i]) for i in range(x_out.shape[0])], sems)
+
+
+def send_c_kernel(n_near, n_slots, k, j, c_in, *refs):
     outs, sems = refs[:n_slots], refs[n_slots]
-    copies = []
+    pairs = []
     for s in range(n_slots):
         if s < n_near:
             for g in range(2):
-                copies.append((source.at[k[0] ^ s, j[0] ^ (2 * g)], outs[s].at[g]))
+                pairs.append((c_in.at[k[0] ^ s, j[0] ^ (2 * g)], outs[s].at[g]))
         else:
-            copies.append((source.at[k[0] ^ s, j[0]], outs[s]))
-    started = [
-        pltpu.make_async_copy(src, dst, sems.at[i]) for i, (src, dst) in enumerate(copies)
-    ]
-    for copy in started:
-        copy.start()
-    for copy in started:
-        copy.wait()
+            pairs.append((c_in.at[k[0] ^ s, j[0]], outs[s]))
+    copy_all(pairs, sems)
+
+
+def stack_kernel(*refs):
+    parts, out = refs[:-1], refs[-1]
+    for i, ref in enumerate(parts):
+        out[i] = ref[...]
+
+
+def kept_row(runs, frames, rows, first):
+    lane = lax.broadcasted_iota(jnp.int32, (frames, frames * rows), 1)
+    frame = lax.broadcasted_iota(jnp.int32, (frames, frames * rows), 0)
+    place = first + lane % rows
+    begins, lengths = runs[:, 0, :], runs[:, 1, :]
+    hits = jnp.zeros((frames, frames * rows), F32)
+    for r in range(begins.shape[1]):
+        begin = begins[:, r : r + 1]
+        here = (place >= begin) & (place < begin + lengths[:, r : r + 1])
+        hits = jnp.where(here, 1.0, hits)
+    return jnp.sum(jnp.where(frame == lane // rows, hits, 0.0), axis=0, keepdims=True)
 
 
 def attend_kernel(
-    frames, rows, picks, who, where, gain, wa, wb, oa, ob, mask, x_in, *refs
+    frames, rows, picks, n_te, g, who, where, gain_in, wa, wb, oa, ob, runs, x_in, *refs
 ):
-    c_in = refs[: len(picks)]
-    c_all, normed, mixed, pcot, keep, send, stats, gains = refs[len(picks) :]
-    for s, (ref, pick) in enumerate(zip(c_in, picks)):
-        if len(picks) == 1:
-            c_all[...] = ref[...]
-        else:
+    c_in, rest = refs[: len(picks)], refs[len(picks) :]
+    c_all, normed, mixed, pcot, keep, send, stats, gains = rest
+    if len(picks) == 1:
+        c_all[...] = c_in[0][...]
+    else:
+        for s, (ref, pick) in enumerate(zip(c_in, picks)):
             c_all[where[0] ^ s] = ref[...] if pick is None else ref[pick]
+    gain = gain_in[...].reshape(1, x_in.shape[2])
     wq, wk, wv = (all_rows((wa[i], wb[i])) for i in range(3))
     wout = all_rows((oa[...], ob[...]))
     width, full = wout.shape
@@ -129,13 +156,18 @@
     tokens = frames * chunk
     n_rows = frames * rows
     standard, _ = standardize(x_in[...].reshape(tokens, full))
-    n = (standard * gain[...]).astype(BF)
+    n = (standard * gain).astype(BF)
     normed[...] = n
     qs, ks, vs = (dot_t(n, w).astype(BF) for w in (wq, wk, wv))
     c = c_all[...].reshape(tokens, full)
     mc = dot_t(c, wout).astype(BF)
+    row = lax.broadcasted_iota(jnp.int32, (n_rows, n_rows), 0)
+    col = lax.broadcasted_iota(jnp.int32, (n_rows, n_rows), 1)
+    first = (where[0] * n_te + (who[0] ^ (2 * g))) * chunk
     for b in range(chunk // rows):
-        inside = mask[b]
+        across = kept_row(runs, frames, rows, first + b * rows)
+        down = jnp.sum(jnp.where(row == col, across, 0.0), axis=1, keepdims=True)
+        inside = jnp.where(row % rows == col % rows, across * down, 0.0)
         for p in range(width // LANES):
             cols = slice(p * LANES, (p + 1) * LANES)
             q, k, v, dm = (block_rows(z[:, cols], frames, b, rows) for z in (qs, ks, vs, mc))
@@ -166,9 +198,9 @@
     pc = pcot[...].reshape(tokens, 3 * width)
     nc = dot(pc, all_rows((wq, wk, wv)))
     nn = n.astype(F32) * nc
-    mean_plain = jnp.sum(nc * gain[...], axis=-1, keepdims=True)
+    mean_plain = jnp.sum(nc * gain, axis=-1, keepdims=True)
     mean_cross = jnp.sum(nn, axis=-1, keepdims=True)
-    total_gain = jnp.sum(nn, axis=0, keepdims=True) / gain[...]
+    total_gain = jnp.sum(nn, axis=0, keepdims=True) / gain
     lane = lax.broadcasted_iota(jnp.int32, (tokens, LANES), 1)
     both = jnp.where(lane == 0, mean_plain, mean_cross) * (1.0 / full)
     half = full // 2
@@ -224,7 +256,7 @@
     proj[...] = b[:, share:].T.astype(BF)
 
 
-def finish_kernel(who, x_in, c_in, gain, keep, recv, stats, stats_in, *refs):
+def finish_kernel(who, x_in, c_in, gain_in, keep, recv, stats, stats_in, *refs):
     tokens = keep.shape[1]
     full = x_in.shape[-1]
     own, swap = refs[-2:] if len(refs) == 2 else refs[3:5]
@@ -233,7 +265,7 @@
     both = (stats[:, :tokens] + stats_in[:, :tokens]).T
     mean_plain, mean_cross = both[:, 0:1], both[:, 1:2]
     out = halves(x.astype(F32), who)[0] + keep[0] + recv[0].astype(F32)
-    scaled = (keep[1] + recv[1].astype(F32)) * halves(gain[...], who)[0]
+    scaled = (keep[1] + recv[1].astype(F32)) * halves(gain_in[...].reshape(1, full), who)[0]
     through = inverse * (scaled - mean_plain - halves(standard, who)[0] * mean_cross)
     back = halves(c_in[...].reshape(tokens, full).astype(F32), who)[0] + through
     for i, value in enumerate((out, back)):
@@ -309,10 +341,13 @@
     value = held[0].astype(F32)
     for s in range(1, n_slots):
         value = value + held[s].astype(F32)
-    total[...] = value
-
-
-def call(kernel, outs, *args, scalars=1, scratch=(), in_hbm=(), out_hbm=()):
+    n_parts = -(-share // lanes)
+    value = value[:n_parts] + value[n_parts : 2 * n_parts]
+    value = jnp.concatenate([value[i : i + 1] for i in range(n_parts)], axis=1)
+    total[...] = value[:, :share]
+
+
+def call(kernel, outs, *args, scalars=1, scratch=(), in_hbm=(), out_hbm=(), limit=None):
     def space(i, hbm):
         return pl.BlockSpec(memory_space=pl.ANY if i in hbm else pltpu.VMEM)
 
@@ -323,7 +358,7 @@
         + [space(i, in_hbm) for i in range(scalars, len(args))],
         out_specs=[space(i, out_hbm) for i in range(len(outs))],
         scratch_shapes=scratch,
-        compiler_params=pltpu.CompilerParams(vmem_limit_bytes=VMEM_LIMIT),
+        compiler_params=pltpu.CompilerParams(vmem_limit_bytes=limit or VMEM_LIMIT),
     )(*args)
 
 
@@ -344,9 +379,7 @@
     half = width // 2
     lanes = n_te * chunk
 
-    w_own = jnp.transpose(w_qkv, (1, 2, 0))
-    matrices = (w_own, exchange(w_own, "tensor", 1), w_out, exchange(w_out, "tensor", 1))
-    gain = norm_gain.reshape(1, width)
+    gain = norm_gain
 
     def gather_chunks(value):
         mine = lax.dynamic_index_in_dim(
@@ -355,48 +388,49 @@
         first = lax.all_to_all(mine, "tm", split_axis=0, concat_axis=0, tiled=True)
         return first, exchange(first, "tensor", 2)
 
-    xs = gather_chunks(frames_in)
+    w_own = jnp.transpose(w_qkv, (1, 2, 0))
+    w_other = exchange(w_own, "tensor", 1)
+    out_other = exchange(w_out, "tensor", 1)
     if direct:
+        (x_mine,) = call(
+            send_x_kernel, [((n_tm, chunk, width), BF)],
+            who, frames_in.reshape(n_tm, n_te, chunk, width),
+            in_hbm=(1,), limit=WHOLE_VMEM,
+            scratch=[pltpu.SemaphoreType.DMA((n_tm,))],
+        )
         parts = call(
-            functools.partial(send_kernel, n_near, n_tm),
+            functools.partial(send_c_kernel, n_near, n_tm),
             [((2, chunk, width), BF)] * n_near + [((chunk, width), BF)] * (n_tm - n_near),
             where, who, out_cotangent.reshape(n_tm, n_te, chunk, width),
-            scalars=2, in_hbm=(2,), out_hbm=range(n_tm),
+            scalars=2, in_hbm=(2,), limit=WHOLE_VMEM,
             scratch=[pltpu.SemaphoreType.DMA((n_tm + n_near,))],
         )
+        first = lax.all_to_all(x_mine, "tm", split_axis=0, concat_axis=0, tiled=True)
+        xs = (first, exchange(first, "tensor", 2))
         far = [exchange(parts[s], "tm", s) for s in range(n_near, n_tm)]
         near = [parts[0]] + [exchange(parts[s], "tm", s) for s in range(1, n_near)]
-        passed = [exchange(part, "tensor", 2) for part in far]
-        cs = (near + far, near + passed)
-        picks = [[g] * n_near + [None] * (n_tm - n_near) for g in range(2)]
+        (stacked,) = call(
+            stack_kernel, [((n_tm - n_near, chunk, width), BF)], *far,
+            scalars=0,
+        )
+        passed = exchange(stacked, "tensor", 2)
+        cs = (near + far, near + [passed] * (n_tm - n_near))
+        picks = [
+            [0] * n_near + [None] * (n_tm - n_near), [1] * n_near + list(range(n_tm - n_near))
+        ]
     else:
+        xs = gather_chunks(frames_in)
         cs = tuple([value] for value in gather_chunks(out_cotangent))
         picks = [[None], [None]]
-
-    starts = keep_runs[:, :, 0]
-    ends = starts + keep_runs[:, :, 1]
-    chunks = jnp.stack([j, j ^ 2])
-    places = (
-        k * (n_te * chunk) + chunks[:, None] * chunk + jnp.arange(chunk, dtype=jnp.int32)[None, :]
-    )
-    kept = jnp.any(
-        (places[:, None, None, :] >= starts[None, :, :, None])
-        & (places[:, None, None, :] < ends[None, :, :, None]),
-        axis=2,
-    )
-    kept = kept.reshape(2, frames, chunk // rows, rows).transpose(0, 2, 1, 3)
-    kept = kept.reshape(2, chunk // rows, frames * rows)
-    place_of = jnp.arange(frames * rows, dtype=jnp.int32) % rows
-    mask = (
-        kept[:, :, :, None] & kept[:, :, None, :] & (place_of[:, None] == place_of[None, :])
-    ).astype(F32)
-
+    matrices = (w_own, w_other, w_out, out_other)
+
+    runs = jnp.transpose(keep_runs, (0, 2, 1))
     cube = (frames, chunk)
     done, recvs, stats_in = [], [], []
     for g in range(2):
         done.append(
             call(
-                functools.partial(attend_kernel, frames, rows, picks[g]),
+                functools.partial(attend_kernel, frames, rows, picks[g], n_te, g),
                 [
                     (cube + (width,), BF),
                     ((tokens, width), BF),
@@ -407,7 +441,7 @@
                     ((8, tokens + -(-half // LANES) * LANES), F32),
                     ((1, half), F32),
                 ],
-                who, where, gain, *matrices, mask[g], xs[g], *cs[g],
+                who, where, gain, *matrices, runs, xs[g], *cs[g],
                 scalars=2,
             )
         )
@@ -476,7 +510,7 @@
         message = lax.all_to_all(message, "tm", split_axis=0, concat_axis=0, tiled=True)
         whole = ((share, place_total), BF)
         block_out, grad_in, total = call(
-            assemble_kernel, [whole, whole, ((extra, lanes), F32)], message,
+            assemble_kernel, [whole, whole, ((1, share), F32)], message,
             scalars=0, in_hbm=(0,), out_hbm=(0, 1),
             scratch=[
                 pltpu.VMEM((n_tm, extra, lanes), BF),
@@ -484,7 +518,7 @@
             ],
         )
         block_out, grad_in = block_out.T, grad_in.T
-        grad_gain = (total[:n_parts] + total[n_parts : 2 * n_parts]).reshape(-1)[:share]
+        grad_gain = total.reshape(share)
     else:
         order = jnp.arange(n_te, dtype=jnp.int32) ^ j
         four = jnp.stack(

time: 132 us -> 126 us (0.955)
  waiting for transfers between devices: 45.9 us -> 63.7 us
  local copies, waits for them, and re-layouts: 13.4 us -> 0.92 us
  starting transfers between devices: 41.1 us -> 34.9 us
  other arithmetic: 5 us -> 0 us
    all_to_all x1, waiting for transfers between devices: 0.01 us -> 11.6 us  [block(): lax.all_to_all(x_mine, 'tm', split_axis=0, concat_axis=0, tiled=True)]
    unnamed x22 -> x14, local copies, waits for them, and re-layouts: 7.31 us -> 0.92 us
    ppermute x27 -> x24, waiting for transfers between devices: 45.9 us -> 52.1 us  [exchange(): return lax.ppermute(value, axis, [(i, i ^ bit) for i in range(size)])]
    ppermute x27 -> x24, starting transfers between devices: 29.6 us -> 23.9 us  [exchange(): return lax.ppermute(value, axis, [(i, i ^ bit) for i in range(size)])]
    reshape x2 -> x0, local copies, waits for them, and re-layouts: 2.04 us -> none  [the longest x1 1.35 us: block(): kept = kept.reshape(2, frames, chunk // rows, rows).transpose(0, 2, 1, 3)]
    reduce_or x1 -> x0, other arithmetic: 1.38 us -> none  [block(): jnp.any((places[:, None, None, :] >= starts[None, :, :, None]) & (places[...]
    and x1 -> x0, local copies, waits for them, and re-layouts: 1.32 us -> none  [block(): kept[:, :, :, None] & kept[:, :, None, :]]
    pallas_call x12 -> x14, Pallas kernels: 24.6 us -> 24.9 us  [call(): pl.pallas_call(kernel, out_shape=[jax.ShapeDtypeStruct(shape, kind) for s...]
  transfers between devices with their start and end apart: 29 -> 26, of which waited for: 14 -> 16; matrix products, arithmetic and copies ran while one was open for 7% -> 0% of each run, Pallas kernels for 13% -> 13%
where the time goes in v2:
time: 126 us; the launch traced here: 125 us
  waiting for transfers between devices  63.7 us (51%)
  starting transfers between devices  34.9 us (28%)
  Pallas kernels  24.9 us (20%)
    ppermute x24, waiting for transfers between devices, exchange(): return lax.ppermute(value, axis, [(i, i ^ bit) for i in range(size)])  52.1 us
    pallas_call x14, Pallas kernels, call(): pl.pallas_call(kernel, out_shape=[jax.ShapeDtypeStruct(shape, kind) for s...  24.9 us
    ppermute x24, starting transfers between devices, exchange(): return lax.ppermute(value, axis, [(i, i ^ bit) for i in range(size)])  23.9 us
    all_to_all x1, waiting for transfers between devices, block(): lax.all_to_all(x_mine, 'tm', split_axis=0, concat_axis=0, tiled=True)  11.6 us
    all_to_all x1, starting transfers between devices, block(): lax.all_to_all(x_mine, 'tm', split_axis=0, concat_axis=0, tiled=True)  7.45 us
    all_to_all x1, starting transfers between devices, block(): lax.all_to_all(message, 'tm', split_axis=0, concat_axis=0, tiled=True)  3.55 us
  transfers between devices with their start and end apart: 26, of which 16 were waited for; matrix products, arithmetic and copies ran while one was open for 0% of the time, Pallas kernels for 13%

profile of v2, /device:TPU:0, one launch (start us, length us, event | category | flops | bytes accessed | tf_op | source)
XLA Modules:
  0.0 125.4 jit_solution(7209313260036335719)
XLA Ops:
  0.6 1.9 %shard_map.101 = bf16[8,32,768]{2,1,0:T(8,128)(2,1)} custom-call(s32[1]{0:T(128)} %bitcast.j.who, bf16[8,4,32,768]{3,2,1,0:T(8,128)(2,1)} %bitcast.34), custom_call_target="tpu_custom_call" | custom-call | tf_op jit(solution)/shard_map/pallas_call | solution.py:354
  2.5 7.5 %all-to-all-start = ((bf16[8,32,768]{2,1,0:T(8,128)(2,1)}), bf16[8,32,768]{2,1,0:T(8,128)(2,1)S(1)}, u32[]{:S(2)}, u32[]{:S(2)}) async-start(bf16[8,32,768]{2,1,0:T(8,128)(2,1)} %shard_map.101), calls=%async_computation | async-start | bytes 786432 | tf_op jit(solution)/shard_map/all_to_all | solution.py:408
  10.1 11.6 %all-to-all-done.x_in = bf16[8,32,768]{2,1,0:T(8,128)(2,1)S(1)} async-done(((bf16[8,32,768]{2,1,0:T(8,128)(2,1)}), bf16[8,32,768]{2,1,0:T(8,128)(2,1)S(1)}, u32[]{:S(2)}, u32[]{:S(2)}) %all-to-all-start) | async-done | bytes 393248 | tf_op jit(solution)/shard_map/all_to_all | solution.py:408
  23.2 2.0 %shard_map.102 = (bf16[2,32,768]{2,1,0:T(8,128)(2,1)}, bf16[2,32,768]{2,1,0:T(8,128)(2,1)}, bf16[2,32,768]{2,1,0:T(8,128)(2,1)}, bf16[2,32,768]{2,1,0:T(8,128)(2...) custom-call(s32[1]{0:T(128)} %bitcast.2.k.where, ...), custom_call_target="tpu_custom_call" | custom-call | tf_op jit(solution)/shard_map/pallas_call | solution.py:354
  26.0 3.1 %collective-permute-start.6 = (bf16[32,768]{1,0:T(8,128)(2,1)}, bf16[32,768]{1,0:T(8,128)(2,1)S(1)}, u32[]{:S(2)}, u32[]{:S(2)}) collective-permute-start(bf16[32,768]{1,0:T(8,128)(2,1)} %get-tuple-element.58), channel_id=1, source_target_pairs={{0,20},{4,16},{8,28},{12,24},{16,4},{20,0},{24,12},{28,8},{1,21},{... | collective-permute-start | bytes 147464 | tf_op jit(solution)/shard_map/ppermute | solution.py:25
  31.7 1.7 %collective-permute-start.2 = (bf16[2,32,768]{2,1,0:T(8,128)(2,1)}, bf16[2,32,768]{2,1,0:T(8,128)(2,1)S(1)}, u32[]{:S(2)}, u32[]{:S(2)}) collective-permute-start(bf16[2,32,768]{2,1,0:T(8,128)(2,1)} %get-tuple-element.54), channel_id=1, source_target_pairs={{0,4},{4,0},{8,12},{12,8},{16,20},{20,16},{24,28},{28,24},{1,5},{5... | collective-permute-start | bytes 294920 | tf_op jit(solution)/shard_map/ppermute | solution.py:25
  33.6 1.5 %collective-permute-done.7.refs_6_.refs_2_ = bf16[32,768]{1,0:T(8,128)(2,1)S(1)} collective-permute-done((bf16[32,768]{1,0:T(8,128)(2,1)}, bf16[32,768]{1,0:T(8,128)(2,1)S(1)}, u32[]{:S(2)}, u32[]{:S(2)}) %collective-permute-start.7) | collective-permute-done | bytes 49184 | tf_op jit(solution)/shard_map/ppermute | solution.py:25
  36.4 5.7 %collective-permute-done.8.refs_7_.refs_3_ = bf16[32,768]{1,0:T(8,128)(2,1)S(1)} collective-permute-done((bf16[32,768]{1,0:T(8,128)(2,1)}, bf16[32,768]{1,0:T(8,128)(2,1)S(1)}, u32[]{:S(2)}, u32[]{:S(2)}) %collective-permute-start.8) | collective-permute-done | bytes 49184 | tf_op jit(solution)/shard_map/ppermute | solution.py:25
  42.8 4.2 %collective-permute-done.3.refs_2_ = bf16[2,32,768]{2,1,0:T(8,128)(2,1)S(1)} collective-permute-done((bf16[2,32,768]{2,1,0:T(8,128)(2,1)}, bf16[2,32,768]{2,1,0:T(8,128)(2,1)S(1)}, u32[]{:S(2)}, u32[]{:S(2)}) %collective-permute-start.3) | collective-permute-done | bytes 98336 | tf_op jit(solution)/shard_map/ppermute | solution.py:25
  46.9 5.7 %collective-permute-done.4.refs_3_ = bf16[2,32,768]{2,1,0:T(8,128)(2,1)S(1)} collective-permute-done((bf16[2,32,768]{2,1,0:T(8,128)(2,1)}, bf16[2,32,768]{2,1,0:T(8,128)(2,1)S(1)}, u32[]{:S(2)}, u32[]{:S(2)}) %collective-permute-start.4) | collective-permute-done | bytes 98336 | tf_op jit(solution)/shard_map/ppermute | solution.py:25
  53.6 5.4 %shard_map.105 = (bf16[8,32,768]{2,1,0:T(8,128)(2,1)S(1)}, bf16[256,768]{1,0:T(8,128)(2,1)S(1)}, bf16[8,32,384]{2,1,0:T(8,128)(2,1)S(1)}, bf16[8,32,1152]{2,1,0:...) custom-call(s32[1]{0:T(128)} %bitcast.j.who, ...), custom_call_target="tpu_custom_call" | custom-call | tf_op jit(solution)/shard_map/pallas_call | solution.py:354
  59.6 5.4 %shard_map.103 = (bf16[8,32,768]{2,1,0:T(8,128)(2,1)S(1)}, bf16[256,768]{1,0:T(8,128)(2,1)S(1)}, bf16[8,32,384]{2,1,0:T(8,128)(2,1)S(1)}, bf16[8,32,1152]{2,1,0:...) custom-call(s32[1]{0:T(128)} %bitcast.j.who, ...), custom_call_target="tpu_custom_call" | custom-call | tf_op jit(solution)/shard_map/pallas_call | solution.py:354
  65.1 1.5 %collective-permute-start.14 = (bf16[2,256,384]{2,1,0:T(8,128)(2,1)S(1)}, bf16[2,256,384]{2,1,0:T(8,128)(2,1)S(1)}, u32[]{:S(2)}, u32[]{:S(2)}) collective-permute-start(bf16[2,256,384]{2,1,0:T(8,128)(2,1)S(1)} %get-tuple-element.71), channel_id=1, source_target_pairs={{0,2},{1,3},{2,0},{3,1},{4,6},{5,7},{6,4},{7,5},{8,10},{9,11},{10,... | collective-permute-start | bytes 1179656 | tf_op jit(solution)/shard_map/ppermute | solution.py:25
  66.6 2.9 %shard_map.110 = (f32[768,768]{1,0:T(8,128)S(1)}, bf16[768,768]{1,0:T(8,128)(2,1)}) custom-call(bf16[256,768]{1,0:T(8,128)(2,1)S(1)} %get-tuple-element.78.n0, bf16[256,768]{1,0:T(8,128)(2,1)S(1)} %get-tuple-element.79.n1, bf16[256,1152]{1,0:T(8,128)(2,1)S(1)} %bitcast.29, bf16[256,1152]{1,0:T(8,128)(2,1)S(1)} %bitcast.28, bf16[256,768]{1,0:T(8,128)(2,1)S(1)} %bitcast.26, ...), custom_call_target="tpu_custom_call" | custom-call | tf_op jit(solution)/shard_map/pallas_call | solution.py:354
  71.5 4.4 %collective-permute-done.13.refs_2_.stats_in = f32[8,640]{1,0:T(8,128)S(1)} collective-permute-done((f32[8,640]{1,0:T(8,128)S(1)}, f32[8,640]{1,0:T(8,128)S(1)}, u32[]{:S(2)}, u32[]{:S(2)}) %collective-permute-start.13) | collective-permute-done | bytes 20512 | tf_op jit(solution)/shard_map/ppermute | solution.py:25
  81.2 3.5 %all-to-all-start.1 = ((bf16[8,400,128]{2,1,0:T(8,128)(2,1)}), bf16[8,400,128]{2,1,0:T(8,128)(2,1)S(1)}, u32[]{:S(2)}, u32[]{:S(2)}) async-start(bf16[8,400,128]{2,1,0:T(8,128)(2,1)} %shard_map.108), calls=%async_computation.1 | async-start | bytes 1638400 | tf_op jit(solution)/shard_map/all_to_all | solution.py:510
  86.3 2.0 %collective-permute-start.18 = (bf16[4,96,384]{2,1,0:T(8,128)(2,1)S(1)}, bf16[4,96,384]{2,1,0:T(8,128)(2,1)S(1)}, u32[]{:S(2)}, u32[]{:S(2)}) collective-permute-start(bf16[4,96,384]{2,1,0:T(8,128)(2,1)S(1)} %get-tuple-element.88), channel_id=1, source_target_pairs={{0,4},{4,0},{8,12},{12,8},{16,20},{20,16},{24,28},{28,24},{1,5},{5... | collective-permute-start | bytes 884744 | tf_op jit(solution)/shard_map/ppermute | solution.py:25
  89.7 13.2 %collective-permute-done.18.refs_2_ = bf16[4,96,384]{2,1,0:T(8,128)(2,1)S(1)} collective-permute-done((bf16[4,96,384]{2,1,0:T(8,128)(2,1)S(1)}, bf16[4,96,384]{2,1,0:T(8,128)(2,1)S(1)}, u32[]{:S(2)}, u32[]{:S(2)}) %collective-permute-start.18) | collective-permute-done | bytes 294944 | tf_op jit(solution)/shard_map/ppermute | solution.py:25
  103.0 4.4 %collective-permute-done.19.refs_3_ = bf16[4,96,384]{2,1,0:T(8,128)(2,1)S(1)} collective-permute-done((bf16[4,96,384]{2,1,0:T(8,128)(2,1)S(1)}, bf16[4,96,384]{2,1,0:T(8,128)(2,1)S(1)}, u32[]{:S(2)}, u32[]{:S(2)}) %collective-permute-start.19) | collective-permute-done | bytes 294944 | tf_op jit(solution)/shard_map/ppermute | solution.py:25
  109.7 3.1 %collective-permute-done.20.refs_2_ = bf16[2,96,384]{2,1,0:T(8,128)(2,1)S(1)} collective-permute-done((bf16[2,96,384]{2,1,0:T(8,128)(2,1)S(1)}, bf16[2,96,384]{2,1,0:T(8,128)(2,1)S(1)}, u32[]{:S(2)}, u32[]{:S(2)}) %collective-permute-start.20) | collective-permute-done | bytes 147488 | tf_op jit(solution)/shard_map/ppermute | solution.py:25
  114.1 1.9 %collective-permute-start.22 = (bf16[1,96,384]{2,1,0:T(8,128)(2,1)S(1)}, bf16[1,96,384]{2,1,0:T(8,128)(2,1)S(1)}, u32[]{:S(2)}, u32[]{:S(2)}) collective-permute-start(bf16[1,96,384]{2,1,0:T(8,128)(2,1)S(1)} %get-tuple-element.96), channel_id=1, source_target_pairs={{0,16},{4,20},{8,24},{12,28},{16,0},{20,4},{24,8},{28,12},{1,17},{... | collective-permute-start | bytes 221192 | tf_op jit(solution)/shard_map/ppermute | solution.py:25
  117.1 4.2 %collective-permute-done.22.moved_a = bf16[1,96,384]{2,1,0:T(8,128)(2,1)S(1)} collective-permute-done((bf16[1,96,384]{2,1,0:T(8,128)(2,1)S(1)}, bf16[1,96,384]{2,1,0:T(8,128)(2,1)S(1)}, u32[]{:S(2)}, u32[]{:S(2)}) %collective-permute-start.22) | collective-permute-done | bytes 73760 | tf_op jit(solution)/shard_map/ppermute | solution.py:25
  121.2 1.6 %collective-permute-done.23.moved_b = bf16[1,96,384]{2,1,0:T(8,128)(2,1)S(1)} collective-permute-done((bf16[1,96,384]{2,1,0:T(8,128)(2,1)S(1)}, bf16[1,96,384]{2,1,0:T(8,128)(2,1)S(1)}, u32[]{:S(2)}, u32[]{:S(2)}) %collective-permute-start.23) | collective-permute-done | bytes 73760 | tf_op jit(solution)/shard_map/ppermute | solution.py:25
  123.6 1.6 %shard_map.109 = (bf16[192,1024]{1,0:T(8,128)(2,1)}, bf16[192,1024]{1,0:T(8,128)(2,1)}, f32[1,192]{1,0:T(1,128)}) custom-call(bf16[8,400,128]{2,1,0:T(8,128)(2,1)S(1)} %all-to-all-done.1.parts), custom_call_target="tpu_custom_call" | custom-call | tf_op jit(solution)/shard_map/pallas_call | solution.py:354
  (56 shorter events, 24.3 us)
Async XLA Ops:
  2.5 19.1 %all-to-all-start = ((bf16[8,32,768]{2,1,0:T(8,128)(2,1)}), bf16[8,32,768]{2,1,0:T(8,128)(2,1)S(1)}, u32[]{:S(2)}, u32[]{:S(2)}) async-start(bf16[8,32,768]{2,1,0:T(8,128)(2,1)} %shard_map.101), calls=%async_computation | async-start | bytes 786432 | tf_op jit(solution)/shard_map/all_to_all | solution.py:408
  10.0 42.7 %collective-permute-start = (bf16[3,192,768]{2,1,0:T(8,128)(2,1)S(1)}, bf16[3,192,768]{2,1,0:T(8,128)(2,1)S(1)}, u32[]{:S(2)}, u32[]{:S(2)}) collective-permute-start(bf16[3,192,768]{2,1,0:T(8,128)(2,1)S(1)} %bitcast.22), channel_id=1, source_target_pairs={{0,1},{1,0},{2,3},{3,2},{4,5},{5,4},{6,7},{7,6},{8,9},{9,8},{10,11... | collective-permute-start | bytes 2654216 | tf_op jit(solution)/shard_map/ppermute | solution.py:25
  21.7 31.0 %collective-permute-start.9 = (bf16[8,32,768]{2,1,0:T(8,128)(2,1)S(1)}, bf16[8,32,768]{2,1,0:T(8,128)(2,1)S(1)}, u32[]{:S(2)}, u32[]{:S(2)}) collective-permute-start(bf16[8,32,768]{2,1,0:T(8,128)(2,1)S(1)} %all-to-all-done.x_in), channel_id=1, source_target_pairs={{0,2},{1,3},{2,0},{3,1},{4,6},{5,7},{6,4},{7,5},{8,10},{9,11},{10,... | collective-permute-start | bytes 1179656 | tf_op jit(solution)/shard_map/ppermute | solution.py:25
  25.1 6.6 %collective-permute-start.5 = (bf16[32,768]{1,0:T(8,128)(2,1)}, bf16[32,768]{1,0:T(8,128)(2,1)S(1)}, u32[]{:S(2)}, u32[]{:S(2)}) collective-permute-start(bf16[32,768]{1,0:T(8,128)(2,1)} %get-tuple-element.57), channel_id=1, source_target_pairs={{0,16},{4,20},{8,24},{12,28},{16,0},{20,4},{24,8},{28,12},{1,17},{... | collective-permute-start | bytes 147464 | tf_op jit(solution)/shard_map/ppermute | solution.py:25
  26.0 7.7 %collective-permute-start.6 = (bf16[32,768]{1,0:T(8,128)(2,1)}, bf16[32,768]{1,0:T(8,128)(2,1)S(1)}, u32[]{:S(2)}, u32[]{:S(2)}) collective-permute-start(bf16[32,768]{1,0:T(8,128)(2,1)} %get-tuple-element.58), channel_id=1, source_target_pairs={{0,20},{4,16},{8,28},{12,24},{16,4},{20,0},{24,12},{28,8},{1,21},{... | collective-permute-start | bytes 147464 | tf_op jit(solution)/shard_map/ppermute | solution.py:25
  29.0 6.1 %collective-permute-start.7 = (bf16[32,768]{1,0:T(8,128)(2,1)}, bf16[32,768]{1,0:T(8,128)(2,1)S(1)}, u32[]{:S(2)}, u32[]{:S(2)}) collective-permute-start(bf16[32,768]{1,0:T(8,128)(2,1)} %get-tuple-element.59), channel_id=1, source_target_pairs={{0,24},{4,28},{8,16},{12,20},{16,8},{20,12},{24,0},{28,4},{1,25},{... | collective-permute-start | bytes 147464 | tf_op jit(solution)/shard_map/ppermute | solution.py:25
  31.7 10.4 %collective-permute-start.2 = (bf16[2,32,768]{2,1,0:T(8,128)(2,1)}, bf16[2,32,768]{2,1,0:T(8,128)(2,1)S(1)}, u32[]{:S(2)}, u32[]{:S(2)}) collective-permute-start(bf16[2,32,768]{2,1,0:T(8,128)(2,1)} %get-tuple-element.54), channel_id=1, source_target_pairs={{0,4},{4,0},{8,12},{12,8},{16,20},{20,16},{24,28},{28,24},{1,5},{5... | collective-permute-start | bytes 294920 | tf_op jit(solution)/shard_map/ppermute | solution.py:25
  33.6 19.1 %collective-permute-start.1 = (bf16[192,768]{1,0:T(8,128)(2,1)S(1)}, bf16[192,768]{1,0:T(8,128)(2,1)S(1)}, u32[]{:S(2)}, u32[]{:S(2)}) collective-permute-start(bf16[192,768]{1,0:T(8,128)(2,1)S(1)} %copy-done.3), channel_id=1, source_target_pairs={{0,1},{1,0},{2,3},{3,2},{4,5},{5,4},{6,7},{7,6},{8,9},{9,8},{10,11... | collective-permute-start | bytes 884744 | tf_op jit(solution)/shard_map/ppermute | solution.py:25
  35.1 7.0 %collective-permute-start.8 = (bf16[32,768]{1,0:T(8,128)(2,1)}, bf16[32,768]{1,0:T(8,128)(2,1)S(1)}, u32[]{:S(2)}, u32[]{:S(2)}) collective-permute-start(bf16[32,768]{1,0:T(8,128)(2,1)} %get-tuple-element.60), channel_id=1, source_target_pairs={{0,28},{4,24},{8,20},{12,16},{16,12},{20,8},{24,4},{28,0},{1,29},{... | collective-permute-start | bytes 147464 | tf_op jit(solution)/shard_map/ppermute | solution.py:25
  42.1 4.8 %collective-permute-start.3 = (bf16[2,32,768]{2,1,0:T(8,128)(2,1)}, bf16[2,32,768]{2,1,0:T(8,128)(2,1)S(1)}, u32[]{:S(2)}, u32[]{:S(2)}) collective-permute-start(bf16[2,32,768]{2,1,0:T(8,128)(2,1)} %get-tuple-element.55), channel_id=1, source_target_pairs={{0,8},{4,12},{8,0},{12,4},{16,24},{20,28},{24,16},{28,20},{1,9},{5... | collective-permute-start | bytes 294920 | tf_op jit(solution)/shard_map/ppermute | solution.py:25
  42.1 10.5 %collective-permute-start.10 = (bf16[4,32,768]{2,1,0:T(8,128)(2,1)S(1)}, bf16[4,32,768]{2,1,0:T(8,128)(2,1)S(1)}, u32[]{:S(2)}, u32[]{:S(2)}) collective-permute-start(bf16[4,32,768]{2,1,0:T(8,128)(2,1)S(1)} %shard_map.104), channel_id=1, source_target_pairs={{0,2},{1,3},{2,0},{3,1},{4,6},{5,7},{6,4},{7,5},{8,10},{9,11},{10,... | collective-permute-start | bytes 589832 | tf_op jit(solution)/shard_map/ppermute | solution.py:25
  46.9 5.7 %collective-permute-start.4 = (bf16[2,32,768]{2,1,0:T(8,128)(2,1)}, bf16[2,32,768]{2,1,0:T(8,128)(2,1)S(1)}, u32[]{:S(2)}, u32[]{:S(2)}) collective-permute-start(bf16[2,32,768]{2,1,0:T(8,128)(2,1)} %get-tuple-element.56), channel_id=1, source_target_pairs={{0,12},{4,8},{8,4},{12,0},{16,28},{20,24},{24,20},{28,16},{1,13},{... | collective-permute-start | bytes 294920 | tf_op jit(solution)/shard_map/ppermute | solution.py:25
  59.1 17.1 %collective-permute-start.11 = (bf16[2,256,384]{2,1,0:T(8,128)(2,1)S(1)}, bf16[2,256,384]{2,1,0:T(8,128)(2,1)S(1)}, u32[]{:S(2)}, u32[]{:S(2)}) collective-permute-start(bf16[2,256,384]{2,1,0:T(8,128)(2,1)S(1)} %get-tuple-element.63), channel_id=1, source_target_pairs={{0,2},{1,3},{2,0},{3,1},{4,6},{5,7},{6,4},{7,5},{8,10},{9,11},{10,... | collective-permute-start | bytes 1179656 | tf_op jit(solution)/shard_map/ppermute | solution.py:25
  65.1 12.2 %collective-permute-start.14 = (bf16[2,256,384]{2,1,0:T(8,128)(2,1)S(1)}, bf16[2,256,384]{2,1,0:T(8,128)(2,1)S(1)}, u32[]{:S(2)}, u32[]{:S(2)}) collective-permute-start(bf16[2,256,384]{2,1,0:T(8,128)(2,1)S(1)} %get-tuple-element.71), channel_id=1, source_target_pairs={{0,2},{1,3},{2,0},{3,1},{4,6},{5,7},{6,4},{7,5},{8,10},{9,11},{10,... | collective-permute-start | bytes 1179656 | tf_op jit(solution)/shard_map/ppermute | solution.py:25
  69.5 15.3 %collective-permute-start.17 = (bf16[768,768]{1,0:T(8,128)(2,1)}, bf16[768,768]{1,0:T(8,128)(2,1)}, u32[]{:S(2)}, u32[]{:S(2)}) collective-permute-start(bf16[768,768]{1,0:T(8,128)(2,1)} %get-tuple-element.85), channel_id=1, source_target_pairs={{0,1},{1,0},{2,3},{3,2},{4,5},{5,4},{6,7},{7,6},{8,9},{9,8},{10,11... | collective-permute-start | bytes 3538952 | tf_op jit(solution)/shard_map/ppermute | solution.py:25
  69.5 6.4 %collective-permute-start.13 = (f32[8,640]{1,0:T(8,128)S(1)}, f32[8,640]{1,0:T(8,128)S(1)}, u32[]{:S(2)}, u32[]{:S(2)}) collective-permute-start(f32[8,640]{1,0:T(8,128)S(1)} %get-tuple-element.64.stats), channel_id=1, source_target_pairs={{0,2},{1,3},{2,0},{3,1},{4,6},{5,7},{6,4},{7,5},{8,10},{9,11},{10,... | collective-permute-start | bytes 61448 | tf_op jit(solution)/shard_map/ppermute | solution.py:25
  70.1 6.1 %collective-permute-start.12 = (f32[8,640]{1,0:T(8,128)S(1)}, f32[8,640]{1,0:T(8,128)S(1)}, u32[]{:S(2)}, u32[]{:S(2)}) collective-permute-start(f32[8,640]{1,0:T(8,128)S(1)} %get-tuple-element.65.stats), channel_id=1, source_target_pairs={{0,2},{1,3},{2,0},{3,1},{4,6},{5,7},{6,4},{7,5},{8,10},{9,11},{10,... | collective-permute-start | bytes 61448 | tf_op jit(solution)/shard_map/ppermute | solution.py:25
  81.2 42.4 %all-to-all-start.1 = ((bf16[8,400,128]{2,1,0:T(8,128)(2,1)}), bf16[8,400,128]{2,1,0:T(8,128)(2,1)S(1)}, u32[]{:S(2)}, u32[]{:S(2)}) async-start(bf16[8,400,128]{2,1,0:T(8,128)(2,1)} %shard_map.108), calls=%async_computation.1 | async-start | bytes 1638400 | tf_op jit(solution)/shard_map/all_to_all | solution.py:510
  86.3 16.7 %collective-permute-start.18 = (bf16[4,96,384]{2,1,0:T(8,128)(2,1)S(1)}, bf16[4,96,384]{2,1,0:T(8,128)(2,1)S(1)}, u32[]{:S(2)}, u32[]{:S(2)}) collective-permute-start(bf16[4,96,384]{2,1,0:T(8,128)(2,1)S(1)} %get-tuple-element.88), channel_id=1, source_target_pairs={{0,4},{4,0},{8,12},{12,8},{16,20},{20,16},{24,28},{28,24},{1,5},{5... | collective-permute-start | bytes 884744 | tf_op jit(solution)/shard_map/ppermute | solution.py:25
  88.2 19.2 %collective-permute-start.19 = (bf16[4,96,384]{2,1,0:T(8,128)(2,1)S(1)}, bf16[4,96,384]{2,1,0:T(8,128)(2,1)S(1)}, u32[]{:S(2)}, u32[]{:S(2)}) collective-permute-start(bf16[4,96,384]{2,1,0:T(8,128)(2,1)S(1)} %get-tuple-element.89), channel_id=1, source_target_pairs={{0,8},{4,12},{8,0},{12,4},{16,24},{20,28},{24,16},{28,20},{1,9},{5... | collective-permute-start | bytes 884744 | tf_op jit(solution)/shard_map/ppermute | solution.py:25
  107.5 5.3 %collective-permute-start.20 = (bf16[2,96,384]{2,1,0:T(8,128)(2,1)S(1)}, bf16[2,96,384]{2,1,0:T(8,128)(2,1)S(1)}, u32[]{:S(2)}, u32[]{:S(2)}) collective-permute-start(bf16[2,96,384]{2,1,0:T(8,128)(2,1)S(1)} %get-tuple-element.92), channel_id=1, source_target_pairs={{0,8},{4,12},{8,0},{12,4},{16,24},{20,28},{24,16},{28,20},{1,9},{5... | collective-permute-start | bytes 442376 | tf_op jit(solution)/shard_map/ppermute | solution.py:25
  108.7 5.3 %collective-permute-start.21 = (bf16[2,96,384]{2,1,0:T(8,128)(2,1)S(1)}, bf16[2,96,384]{2,1,0:T(8,128)(2,1)S(1)}, u32[]{:S(2)}, u32[]{:S(2)}) collective-permute-start(bf16[2,96,384]{2,1,0:T(8,128)(2,1)S(1)} %get-tuple-element.93), channel_id=1, source_target_pairs={{0,4},{4,0},{8,12},{12,8},{16,20},{20,16},{24,28},{28,24},{1,5},{5... | collective-permute-start | bytes 442376 | tf_op jit(solution)/shard_map/ppermute | solution.py:25
  114.1 7.2 %collective-permute-start.22 = (bf16[1,96,384]{2,1,0:T(8,128)(2,1)S(1)}, bf16[1,96,384]{2,1,0:T(8,128)(2,1)S(1)}, u32[]{:S(2)}, u32[]{:S(2)}) collective-permute-start(bf16[1,96,384]{2,1,0:T(8,128)(2,1)S(1)} %get-tuple-element.96), channel_id=1, source_target_pairs={{0,16},{4,20},{8,24},{12,28},{16,0},{20,4},{24,8},{28,12},{1,17},{... | collective-permute-start | bytes 221192 | tf_op jit(solution)/shard_map/ppermute | solution.py:25
  115.9 6.9 %collective-permute-start.23 = (bf16[1,96,384]{2,1,0:T(8,128)(2,1)S(1)}, bf16[1,96,384]{2,1,0:T(8,128)(2,1)S(1)}, u32[]{:S(2)}, u32[]{:S(2)}) collective-permute-start(bf16[1,96,384]{2,1,0:T(8,128)(2,1)S(1)} %get-tuple-element.97), channel_id=1, source_target_pairs={{0,16},{4,20},{8,24},{12,28},{16,0},{20,4},{24,8},{28,12},{1,17},{... | collective-permute-start | bytes 221192 | tf_op jit(solution)/shard_map/ppermute | solution.py:25
  (9 other events, 159.6 us)

commit v3 on v2

--- a/solution.py
+++ b/solution.py
@@ -284,15 +284,16 @@
         swap[2 * tokens :] = jnp.where(row == 0, top, jnp.where(row == 1, rest, 0.0)).astype(BF)
 
 
-def pack_kernel(frames, who, own_a, own_b, recv_a, recv_b, own_gain, out, held):
+def pack_kernel(frames, who, where, own_a, own_b, recv_a, recv_b, own_gain, *refs):
+    outs, held = refs[:frames], refs[frames]
     tokens, share = own_a.shape[1:]
     chunk = tokens // frames
+    lanes = outs[0].shape[1]
     j = who[0]
     top = recv_a[2 * tokens : 2 * tokens + 2].astype(F32)
     value = own_gain[...] + top[:1] + top[1:]
-    lanes = out.shape[2]
     n_parts = -(-share // lanes)
-    extra = out.shape[1] - 2 * share
+    extra = outs[0].shape[0] - 2 * share
     block = jnp.zeros((extra, lanes), F32)
     at = lax.broadcasted_iota(jnp.int32, (extra, lanes), 0)
     row = 0
@@ -302,49 +303,42 @@
         for i in range(n_parts):
             block = jnp.where(at == row, part[:, i * lanes : (i + 1) * lanes], block)
             row += 1
-    for i in range(2):
-        for s in range(frames):
-            rows = slice(s * chunk, (s + 1) * chunk)
-            sent = slice(i * tokens + s * chunk, i * tokens + (s + 1) * chunk)
+    for s in range(frames):
+        frame = where[0] ^ s
+        rows = pl.ds(pl.multiple_of(frame * chunk, chunk), chunk)
+        for i in range(2):
+            sent = pl.ds(pl.multiple_of(i * tokens + frame * chunk, chunk), chunk)
             held[i, s, j] = own_a[i, rows].astype(F32)
             held[i, s, j ^ 2] = own_b[i, rows].astype(F32)
             held[i, s, j ^ 1] = recv_a[sent].astype(F32)
             held[i, s, j ^ 3] = recv_b[sent].astype(F32)
             turned = held[i, s].reshape(4 * chunk, share).T.astype(BF)
-            out[s, i * share : (i + 1) * share] = turned
-    for s in range(frames):
-        out[s, 2 * share :] = block.astype(BF)
-
-
-def assemble_kernel(parts, first, second, total, held, sems):
-    n_slots, rows, lanes = parts.shape
+            outs[s][i * share : (i + 1) * share] = turned
+        outs[s][2 * share :] = block.astype(BF)
+
+
+def assemble_kernel(n_slots, where, *refs):
+    parts = refs[:n_slots]
+    first, second, total, sems = refs[n_slots:]
+    _, lanes = parts[0].shape
     share = first.shape[0]
-    copies = []
-    for i, out in enumerate((first, second)):
-        for s in range(n_slots):
-            copies.append(
-                pltpu.make_async_copy(
-                    parts.at[s, pl.ds(i * share, share)],
-                    out.at[:, pl.ds(s * lanes, lanes)],
-                    sems.at[i * n_slots + s],
-                )
-            )
-    copies.append(
-        pltpu.make_async_copy(
-            parts.at[:, pl.ds(2 * share, rows - 2 * share)], held, sems.at[2 * n_slots]
-        )
-    )
+    pairs = []
+    for s, part in enumerate(parts):
+        at = pl.ds(pl.multiple_of((where[0] ^ s) * lanes, lanes), lanes)
+        for i, out in enumerate((first, second)):
+            pairs.append((part.at[pl.ds(i * share, share)], out.at[:, at]))
+    copies = [pltpu.make_async_copy(src, dst, sems.at[i]) for i, (src, dst) in enumerate(pairs)]
     for copy in copies:
         copy.start()
-    for copy in copies:
-        copy.wait()
-    value = held[0].astype(F32)
-    for s in range(1, n_slots):
-        value = value + held[s].astype(F32)
+    value = parts[0][2 * share :].astype(F32)
+    for part in parts[1:]:
+        value = value + part[2 * share :].astype(F32)
     n_parts = -(-share // lanes)
     value = value[:n_parts] + value[n_parts : 2 * n_parts]
     value = jnp.concatenate([value[i : i + 1] for i in range(n_parts)], axis=1)
     total[...] = value[:, :share]
+    for copy in copies:
+        copy.wait()
 
 
 def call(kernel, outs, *args, scalars=1, scratch=(), in_hbm=(), out_hbm=(), limit=None):
@@ -501,21 +495,19 @@
     if direct:
         n_parts = -(-share // lanes)
         extra = -(-2 * n_parts // 16) * 16
-        (message,) = call(
+        messages = call(
             functools.partial(pack_kernel, frames),
-            [((frames, 2 * share + extra, lanes), BF)],
-            who, *owns, *swapped, own_gain,
+            [((2 * share + extra, lanes), BF)] * frames,
+            who, where, *owns, *swapped, own_gain,
+            scalars=2,
             scratch=[pltpu.VMEM((2, frames, n_te, chunk, share), F32)],
         )
-        message = lax.all_to_all(message, "tm", split_axis=0, concat_axis=0, tiled=True)
+        messages = [messages[0]] + [exchange(messages[s], "tm", s) for s in range(1, n_tm)]
         whole = ((share, place_total), BF)
         block_out, grad_in, total = call(
-            assemble_kernel, [whole, whole, ((1, share), F32)], message,
-            scalars=0, in_hbm=(0,), out_hbm=(0, 1),
-            scratch=[
-                pltpu.VMEM((n_tm, extra, lanes), BF),
-                pltpu.SemaphoreType.DMA((2 * n_tm + 1,)),
-            ],
+            functools.partial(assemble_kernel, n_tm),
+            [whole, whole, ((1, share), F32)], where, *messages,
+            out_hbm=(0, 1), scratch=[pltpu.SemaphoreType.DMA((2 * n_tm,))],
         )
         block_out, grad_in = block_out.T, grad_in.T
         grad_gain = total.reshape(share)

time: 126 us -> 130 us (1.032)
  waiting for transfers between devices: 63.7 us -> 72.9 us
  Pallas kernels: 24.9 us -> 21.7 us
  starting transfers between devices: 34.9 us -> 33.3 us
    ppermute x24 -> x31, waiting for transfers between devices: 52.1 us -> 61.3 us  [exchange(): return lax.ppermute(value, axis, [(i, i ^ bit) for i in range(size)])]
    all_to_all x1 -> x0, starting transfers between devices: 3.55 us -> none  [block(): lax.all_to_all(message, 'tm', split_axis=0, concat_axis=0, tiled=True)]
    pallas_call x14, Pallas kernels: 24.9 us -> 21.7 us  [call(): pl.pallas_call(kernel, out_shape=[jax.ShapeDtypeStruct(shape, kind) for s...]
    ppermute x24 -> x31, starting transfers between devices: 23.9 us -> 25.8 us  [exchange(): return lax.ppermute(value, axis, [(i, i ^ bit) for i in range(size)])]
  transfers between devices with their start and end apart: 26 -> 32, of which waited for: 16 -> 17; matrix products, arithmetic and copies ran while one was open for 0% -> 0% of each run, Pallas kernels for 13% -> 9%
where the time goes in v3:
time: 130 us
  waiting for transfers between devices  72.9 us (56%)
  starting transfers between devices  33.3 us (26%)
  Pallas kernels  21.7 us (17%)
    ppermute x31, waiting for transfers between devices, exchange(): return lax.ppermute(value, axis, [(i, i ^ bit) for i in range(size)])  61.3 us
    ppermute x31, starting transfers between devices, exchange(): return lax.ppermute(value, axis, [(i, i ^ bit) for i in range(size)])  25.8 us
    pallas_call x14, Pallas kernels, call(): pl.pallas_call(kernel, out_shape=[jax.ShapeDtypeStruct(shape, kind) for s...  21.7 us
    all_to_all x1, waiting for transfers between devices, block(): lax.all_to_all(x_mine, 'tm', split_axis=0, concat_axis=0, tiled=True)  11.6 us
    all_to_all x1, starting transfers between devices, block(): lax.all_to_all(x_mine, 'tm', split_axis=0, concat_axis=0, tiled=True)  7.45 us
  transfers between devices with their start and end apart: 32, of which 17 were waited for; matrix products, arithmetic and copies ran while one was open for 0% of the time, Pallas kernels for 9%

profile of v3, /device:TPU:0, one launch (start us, length us, event | category | flops | bytes accessed | tf_op | source)
XLA Modules:
  0.0 129.6 jit_solution(5409387328867599483)
XLA Ops:
  0.6 1.9 %shard_map.101 = bf16[8,32,768]{2,1,0:T(8,128)(2,1)} custom-call(s32[1]{0:T(128)} %bitcast.1.j.who, bf16[8,4,32,768]{3,2,1,0:T(8,128)(2,1)} %bitcast.35), custom_call_target="tpu_custom_call" | custom-call | tf_op jit(solution)/shard_map/pallas_call | solution.py:348
  2.5 7.5 %all-to-all-start = ((bf16[8,32,768]{2,1,0:T(8,128)(2,1)}), bf16[8,32,768]{2,1,0:T(8,128)(2,1)S(1)}, u32[]{:S(2)}, u32[]{:S(2)}) async-start(bf16[8,32,768]{2,1,0:T(8,128)(2,1)} %shard_map.101), calls=%async_computation | async-start | bytes 786432 | tf_op jit(solution)/shard_map/all_to_all | solution.py:402
  10.1 11.6 %all-to-all-done.x_in = bf16[8,32,768]{2,1,0:T(8,128)(2,1)S(1)} async-done(((bf16[8,32,768]{2,1,0:T(8,128)(2,1)}), bf16[8,32,768]{2,1,0:T(8,128)(2,1)S(1)}, u32[]{:S(2)}, u32[]{:S(2)}) %all-to-all-start) | async-done | bytes 393248 | tf_op jit(solution)/shard_map/all_to_all | solution.py:402
  23.2 2.0 %shard_map.102 = (bf16[2,32,768]{2,1,0:T(8,128)(2,1)}, bf16[2,32,768]{2,1,0:T(8,128)(2,1)}, bf16[2,32,768]{2,1,0:T(8,128)(2,1)}, bf16[2,32,768]{2,1,0:T(8,128)(2...) custom-call(s32[1]{0:T(128)} %bitcast.k.where, ...), custom_call_target="tpu_custom_call" | custom-call | tf_op jit(solution)/shard_map/pallas_call | solution.py:348
  26.0 3.1 %collective-permute-start.6 = (bf16[32,768]{1,0:T(8,128)(2,1)}, bf16[32,768]{1,0:T(8,128)(2,1)S(1)}, u32[]{:S(2)}, u32[]{:S(2)}) collective-permute-start(bf16[32,768]{1,0:T(8,128)(2,1)} %get-tuple-element.66), channel_id=1, source_target_pairs={{0,20},{4,16},{8,28},{12,24},{16,4},{20,0},{24,12},{28,8},{1,21},{... | collective-permute-start | bytes 147464 | tf_op jit(solution)/shard_map/ppermute | solution.py:25
  31.8 1.9 %collective-permute-done.6.refs_5_.refs_1_ = bf16[32,768]{1,0:T(8,128)(2,1)S(1)} collective-permute-done((bf16[32,768]{1,0:T(8,128)(2,1)}, bf16[32,768]{1,0:T(8,128)(2,1)S(1)}, u32[]{:S(2)}, u32[]{:S(2)}) %collective-permute-start.6) | collective-permute-done | bytes 49184 | tf_op jit(solution)/shard_map/ppermute | solution.py:25
  35.1 1.7 %collective-permute-start.8 = (bf16[32,768]{1,0:T(8,128)(2,1)}, bf16[32,768]{1,0:T(8,128)(2,1)S(1)}, u32[]{:S(2)}, u32[]{:S(2)}) collective-permute-start(bf16[32,768]{1,0:T(8,128)(2,1)} %get-tuple-element.68), channel_id=1, source_target_pairs={{0,28},{4,24},{8,20},{12,16},{16,12},{20,8},{24,4},{28,0},{1,29},{... | collective-permute-start | bytes 147464 | tf_op jit(solution)/shard_map/ppermute | solution.py:25
  36.9 5.6 %collective-permute-done.8.refs_7_.refs_3_ = bf16[32,768]{1,0:T(8,128)(2,1)S(1)} collective-permute-done((bf16[32,768]{1,0:T(8,128)(2,1)}, bf16[32,768]{1,0:T(8,128)(2,1)S(1)}, u32[]{:S(2)}, u32[]{:S(2)}) %collective-permute-start.8) | collective-permute-done | bytes 49184 | tf_op jit(solution)/shard_map/ppermute | solution.py:25
  43.1 5.0 %collective-permute-done.3.refs_2_ = bf16[2,32,768]{2,1,0:T(8,128)(2,1)S(1)} collective-permute-done((bf16[2,32,768]{2,1,0:T(8,128)(2,1)}, bf16[2,32,768]{2,1,0:T(8,128)(2,1)S(1)}, u32[]{:S(2)}, u32[]{:S(2)}) %collective-permute-start.3) | collective-permute-done | bytes 98336 | tf_op jit(solution)/shard_map/ppermute | solution.py:25
  48.1 5.7 %collective-permute-done.4.refs_3_ = bf16[2,32,768]{2,1,0:T(8,128)(2,1)S(1)} collective-permute-done((bf16[2,32,768]{2,1,0:T(8,128)(2,1)}, bf16[2,32,768]{2,1,0:T(8,128)(2,1)S(1)}, u32[]{:S(2)}, u32[]{:S(2)}) %collective-permute-start.4) | collective-permute-done | bytes 98336 | tf_op jit(solution)/shard_map/ppermute | solution.py:25
  54.8 5.4 %shard_map.103 = (bf16[8,32,768]{2,1,0:T(8,128)(2,1)S(1)}, bf16[256,768]{1,0:T(8,128)(2,1)S(1)}, bf16[8,32,384]{2,1,0:T(8,128)(2,1)S(1)}, bf16[8,32,1152]{2,1,0:...) custom-call(s32[1]{0:T(128)} %bitcast.1.j.who, ...), custom_call_target="tpu_custom_call" | custom-call | tf_op jit(solution)/shard_map/pallas_call | solution.py:348
  60.2 5.5 %shard_map.105 = (bf16[8,32,768]{2,1,0:T(8,128)(2,1)S(1)}, bf16[256,768]{1,0:T(8,128)(2,1)S(1)}, bf16[8,32,384]{2,1,0:T(8,128)(2,1)S(1)}, bf16[8,32,1152]{2,1,0:...) custom-call(s32[1]{0:T(128)} %bitcast.1.j.who, ...), custom_call_target="tpu_custom_call" | custom-call | tf_op jit(solution)/shard_map/pallas_call | solution.py:348
  65.7 1.9 %shard_map.110 = (f32[768,768]{1,0:T(8,128)S(1)}, bf16[768,768]{1,0:T(8,128)(2,1)S(1)}) custom-call(bf16[256,768]{1,0:T(8,128)(2,1)S(1)} %get-tuple-element.94.n0, bf16[256,768]{1,0:T(8,128)(2,1)S(1)} %get-tuple-element.95.n1, bf16[256,1152]{1,0:T(8,128)(2,1)S(1)} %bitcast.29, bf16[256,1152]{1,0:T(8,128)(2,1)S(1)} %bitcast.30, ...), custom_call_target="tpu_custom_call" | custom-call | tf_op jit(solution)/shard_map/pallas_call | solution.py:348
  71.9 16.2 %collective-permute-done.13.refs_2_.stats_in = f32[8,640]{1,0:T(8,128)S(1)} collective-permute-done((f32[8,640]{1,0:T(8,128)S(1)}, f32[8,640]{1,0:T(8,128)S(1)}, u32[]{:S(2)}, u32[]{:S(2)}) %collective-permute-start.13) | collective-permute-done | bytes 20512 | tf_op jit(solution)/shard_map/ppermute | solution.py:25
  88.6 3.3 %collective-permute-done.12.stats_in = f32[8,640]{1,0:T(8,128)S(1)} collective-permute-done((f32[8,640]{1,0:T(8,128)S(1)}, f32[8,640]{1,0:T(8,128)S(1)}, u32[]{:S(2)}, u32[]{:S(2)}) %collective-permute-start.12) | collective-permute-done | bytes 20512 | tf_op jit(solution)/shard_map/ppermute | solution.py:25
  96.8 1.6 %collective-permute-start.28 = (bf16[2,96,384]{2,1,0:T(8,128)(2,1)S(1)}, bf16[2,96,384]{2,1,0:T(8,128)(2,1)S(1)}, u32[]{:S(2)}, u32[]{:S(2)}) collective-permute-start(bf16[2,96,384]{2,1,0:T(8,128)(2,1)S(1)} %get-tuple-element.109), channel_id=1, source_target_pairs={{0,4},{4,0},{8,12},{12,8},{16,20},{20,16},{24,28},{28,24},{1,5},{5... | collective-permute-start | bytes 442376 | tf_op jit(solution)/shard_map/ppermute | solution.py:25
  98.4 1.9 %collective-permute-start.18 = (bf16[400,128]{1,0:T(8,128)(2,1)S(1)}, bf16[400,128]{1,0:T(8,128)(2,1)S(1)}, u32[]{:S(2)}, u32[]{:S(2)}) collective-permute-start(bf16[400,128]{1,0:T(8,128)(2,1)S(1)} %get-tuple-element.86), channel_id=1, source_target_pairs={{0,8},{4,12},{8,0},{12,4},{16,24},{20,28},{24,16},{28,20},{1,9},{5... | collective-permute-start | bytes 307208 | tf_op jit(solution)/shard_map/ppermute | solution.py:25
  102.1 4.2 %collective-permute-done.18.refs_2_ = bf16[400,128]{1,0:T(8,128)(2,1)S(1)} collective-permute-done((bf16[400,128]{1,0:T(8,128)(2,1)S(1)}, bf16[400,128]{1,0:T(8,128)(2,1)S(1)}, u32[]{:S(2)}, u32[]{:S(2)}) %collective-permute-start.18) | collective-permute-done | bytes 102432 | tf_op jit(solution)/shard_map/ppermute | solution.py:25
  106.3 1.7 %collective-permute-start.21 = (bf16[400,128]{1,0:T(8,128)(2,1)S(1)}, bf16[400,128]{1,0:T(8,128)(2,1)S(1)}, u32[]{:S(2)}, u32[]{:S(2)}) collective-permute-start(bf16[400,128]{1,0:T(8,128)(2,1)S(1)} %get-tuple-element.89), channel_id=1, source_target_pairs={{0,20},{4,16},{8,28},{12,24},{16,4},{20,0},{24,12},{28,8},{1,21},{... | collective-permute-start | bytes 307208 | tf_op jit(solution)/shard_map/ppermute | solution.py:25
  108.1 2.6 %collective-permute-start.22 = (bf16[400,128]{1,0:T(8,128)(2,1)S(1)}, bf16[400,128]{1,0:T(8,128)(2,1)S(1)}, u32[]{:S(2)}, u32[]{:S(2)}) collective-permute-start(bf16[400,128]{1,0:T(8,128)(2,1)S(1)} %get-tuple-element.90), channel_id=1, source_target_pairs={{0,24},{4,28},{8,16},{12,20},{16,8},{20,12},{24,0},{28,4},{1,25},{... | collective-permute-start | bytes 307208 | tf_op jit(solution)/shard_map/ppermute | solution.py:25
  110.7 2.0 %collective-permute-start.23 = (bf16[400,128]{1,0:T(8,128)(2,1)S(1)}, bf16[400,128]{1,0:T(8,128)(2,1)S(1)}, u32[]{:S(2)}, u32[]{:S(2)}) collective-permute-start(bf16[400,128]{1,0:T(8,128)(2,1)S(1)} %get-tuple-element.91), channel_id=1, source_target_pairs={{0,28},{4,24},{8,20},{12,16},{16,12},{20,8},{24,4},{28,0},{1,29},{... | collective-permute-start | bytes 307208 | tf_op jit(solution)/shard_map/ppermute | solution.py:25
  112.8 5.8 %collective-permute-done.20.refs_4_ = bf16[400,128]{1,0:T(8,128)(2,1)S(1)} collective-permute-done((bf16[400,128]{1,0:T(8,128)(2,1)S(1)}, bf16[400,128]{1,0:T(8,128)(2,1)S(1)}, u32[]{:S(2)}, u32[]{:S(2)}) %collective-permute-start.20) | collective-permute-done | bytes 102432 | tf_op jit(solution)/shard_map/ppermute | solution.py:25
  118.7 3.9 %collective-permute-done.21.refs_5_ = bf16[400,128]{1,0:T(8,128)(2,1)S(1)} collective-permute-done((bf16[400,128]{1,0:T(8,128)(2,1)S(1)}, bf16[400,128]{1,0:T(8,128)(2,1)S(1)}, u32[]{:S(2)}, u32[]{:S(2)}) %collective-permute-start.21) | collective-permute-done | bytes 102432 | tf_op jit(solution)/shard_map/ppermute | solution.py:25
  124.1 3.5 %collective-permute-done.29.moved_a = bf16[1,96,384]{2,1,0:T(8,128)(2,1)S(1)} collective-permute-done((bf16[1,96,384]{2,1,0:T(8,128)(2,1)S(1)}, bf16[1,96,384]{2,1,0:T(8,128)(2,1)S(1)}, u32[]{:S(2)}, u32[]{:S(2)}) %collective-permute-start.29) | collective-permute-done | bytes 73760 | tf_op jit(solution)/shard_map/ppermute | solution.py:25
  (64 shorter events, 23.3 us)
Async XLA Ops:
  2.5 19.1 %all-to-all-start = ((bf16[8,32,768]{2,1,0:T(8,128)(2,1)}), bf16[8,32,768]{2,1,0:T(8,128)(2,1)S(1)}, u32[]{:S(2)}, u32[]{:S(2)}) async-start(bf16[8,32,768]{2,1,0:T(8,128)(2,1)} %shard_map.101), calls=%async_computation | async-start | bytes 786432 | tf_op jit(solution)/shard_map/all_to_all | solution.py:402
  10.0 43.9 %collective-permute-start = (bf16[3,192,768]{2,1,0:T(8,128)(2,1)S(1)}, bf16[3,192,768]{2,1,0:T(8,128)(2,1)S(1)}, u32[]{:S(2)}, u32[]{:S(2)}) collective-permute-start(bf16[3,192,768]{2,1,0:T(8,128)(2,1)S(1)} %bitcast.22), channel_id=1, source_target_pairs={{0,1},{1,0},{2,3},{3,2},{4,5},{5,4},{6,7},{7,6},{8,9},{9,8},{10,11... | collective-permute-start | bytes 2654216 | tf_op jit(solution)/shard_map/ppermute | solution.py:25
  21.7 38.6 %collective-permute-start.9 = (bf16[8,32,768]{2,1,0:T(8,128)(2,1)S(1)}, bf16[8,32,768]{2,1,0:T(8,128)(2,1)S(1)}, u32[]{:S(2)}, u32[]{:S(2)}) collective-permute-start(bf16[8,32,768]{2,1,0:T(8,128)(2,1)S(1)} %all-to-all-done.x_in), channel_id=1, source_target_pairs={{0,2},{1,3},{2,0},{3,1},{4,6},{5,7},{6,4},{7,5},{8,10},{9,11},{10,... | collective-permute-start | bytes 1179656 | tf_op jit(solution)/shard_map/ppermute | solution.py:25
  25.1 6.6 %collective-permute-start.5 = (bf16[32,768]{1,0:T(8,128)(2,1)}, bf16[32,768]{1,0:T(8,128)(2,1)S(1)}, u32[]{:S(2)}, u32[]{:S(2)}) collective-permute-start(bf16[32,768]{1,0:T(8,128)(2,1)} %get-tuple-element.65), channel_id=1, source_target_pairs={{0,16},{4,20},{8,24},{12,28},{16,0},{20,4},{24,8},{28,12},{1,17},{... | collective-permute-start | bytes 147464 | tf_op jit(solution)/shard_map/ppermute | solution.py:25
  26.0 7.7 %collective-permute-start.6 = (bf16[32,768]{1,0:T(8,128)(2,1)}, bf16[32,768]{1,0:T(8,128)(2,1)S(1)}, u32[]{:S(2)}, u32[]{:S(2)}) collective-permute-start(bf16[32,768]{1,0:T(8,128)(2,1)} %get-tuple-element.66), channel_id=1, source_target_pairs={{0,20},{4,16},{8,28},{12,24},{16,4},{20,0},{24,12},{28,8},{1,21},{... | collective-permute-start | bytes 147464 | tf_op jit(solution)/shard_map/ppermute | solution.py:25
  31.7 22.1 %collective-permute-start.1 = (bf16[192,768]{1,0:T(8,128)(2,1)S(1)}, bf16[192,768]{1,0:T(8,128)(2,1)S(1)}, u32[]{:S(2)}, u32[]{:S(2)}) collective-permute-start(bf16[192,768]{1,0:T(8,128)(2,1)S(1)} %copy-done.1), channel_id=1, source_target_pairs={{0,1},{1,0},{2,3},{3,2},{4,5},{5,4},{6,7},{7,6},{8,9},{9,8},{10,11... | collective-permute-start | bytes 884744 | tf_op jit(solution)/shard_map/ppermute | solution.py:25
  33.6 8.9 %collective-permute-start.2 = (bf16[2,32,768]{2,1,0:T(8,128)(2,1)}, bf16[2,32,768]{2,1,0:T(8,128)(2,1)S(1)}, u32[]{:S(2)}, u32[]{:S(2)}) collective-permute-start(bf16[2,32,768]{2,1,0:T(8,128)(2,1)} %get-tuple-element.62), channel_id=1, source_target_pairs={{0,4},{4,0},{8,12},{12,8},{16,20},{20,16},{24,28},{28,24},{1,5},{5... | collective-permute-start | bytes 294920 | tf_op jit(solution)/shard_map/ppermute | solution.py:25
  35.1 7.3 %collective-permute-start.8 = (bf16[32,768]{1,0:T(8,128)(2,1)}, bf16[32,768]{1,0:T(8,128)(2,1)S(1)}, u32[]{:S(2)}, u32[]{:S(2)}) collective-permute-start(bf16[32,768]{1,0:T(8,128)(2,1)} %get-tuple-element.68), channel_id=1, source_target_pairs={{0,28},{4,24},{8,20},{12,16},{16,12},{20,8},{24,4},{28,0},{1,29},{... | collective-permute-start | bytes 147464 | tf_op jit(solution)/shard_map/ppermute | solution.py:25
  42.5 17.7 %collective-permute-start.10 = (bf16[4,32,768]{2,1,0:T(8,128)(2,1)S(1)}, bf16[4,32,768]{2,1,0:T(8,128)(2,1)S(1)}, u32[]{:S(2)}, u32[]{:S(2)}) collective-permute-start(bf16[4,32,768]{2,1,0:T(8,128)(2,1)S(1)} %shard_map.104), channel_id=1, source_target_pairs={{0,2},{1,3},{2,0},{3,1},{4,6},{5,7},{6,4},{7,5},{8,10},{9,11},{10,... | collective-permute-start | bytes 589832 | tf_op jit(solution)/shard_map/ppermute | solution.py:25
  67.7 24.2 %collective-permute-start.11 = (bf16[2,256,384]{2,1,0:T(8,128)(2,1)S(1)}, bf16[2,256,384]{2,1,0:T(8,128)(2,1)S(1)}, u32[]{:S(2)}, u32[]{:S(2)}) collective-permute-start(bf16[2,256,384]{2,1,0:T(8,128)(2,1)S(1)} %get-tuple-element.71), channel_id=1, source_target_pairs={{0,2},{1,3},{2,0},{3,1},{4,6},{5,7},{6,4},{7,5},{8,10},{9,11},{10,... | collective-permute-start | bytes 1179656 | tf_op jit(solution)/shard_map/ppermute | solution.py:25
  68.3 24.7 %collective-permute-start.14 = (bf16[2,256,384]{2,1,0:T(8,128)(2,1)S(1)}, bf16[2,256,384]{2,1,0:T(8,128)(2,1)S(1)}, u32[]{:S(2)}, u32[]{:S(2)}) collective-permute-start(bf16[2,256,384]{2,1,0:T(8,128)(2,1)S(1)} %get-tuple-element.79), channel_id=1, source_target_pairs={{0,2},{1,3},{2,0},{3,1},{4,6},{5,7},{6,4},{7,5},{8,10},{9,11},{10,... | collective-permute-start | bytes 1179656 | tf_op jit(solution)/shard_map/ppermute | solution.py:25
  70.7 25.4 %collective-permute-start.25 = (bf16[4,96,384]{2,1,0:T(8,128)(2,1)S(1)}, bf16[4,96,384]{2,1,0:T(8,128)(2,1)S(1)}, u32[]{:S(2)}, u32[]{:S(2)}) collective-permute-start(bf16[4,96,384]{2,1,0:T(8,128)(2,1)S(1)} %get-tuple-element.104), channel_id=1, source_target_pairs={{0,4},{4,0},{8,12},{12,8},{16,20},{20,16},{24,28},{28,24},{1,5},{5... | collective-permute-start | bytes 884744 | tf_op jit(solution)/shard_map/ppermute | solution.py:25
  70.8 25.3 %collective-permute-start.26 = (bf16[4,96,384]{2,1,0:T(8,128)(2,1)S(1)}, bf16[4,96,384]{2,1,0:T(8,128)(2,1)S(1)}, u32[]{:S(2)}, u32[]{:S(2)}) collective-permute-start(bf16[4,96,384]{2,1,0:T(8,128)(2,1)S(1)} %get-tuple-element.105), channel_id=1, source_target_pairs={{0,8},{4,12},{8,0},{12,4},{16,24},{20,28},{24,16},{28,20},{1,9},{5... | collective-permute-start | bytes 884744 | tf_op jit(solution)/shard_map/ppermute | solution.py:25
  71.3 16.7 %collective-permute-start.13 = (f32[8,640]{1,0:T(8,128)S(1)}, f32[8,640]{1,0:T(8,128)S(1)}, u32[]{:S(2)}, u32[]{:S(2)}) collective-permute-start(f32[8,640]{1,0:T(8,128)S(1)} %get-tuple-element.72.stats), channel_id=1, source_target_pairs={{0,2},{1,3},{2,0},{3,1},{4,6},{5,7},{6,4},{7,5},{8,10},{9,11},{10,... | collective-permute-start | bytes 61448 | tf_op jit(solution)/shard_map/ppermute | solution.py:25
  96.2 11.9 %collective-permute-start.27 = (bf16[2,96,384]{2,1,0:T(8,128)(2,1)S(1)}, bf16[2,96,384]{2,1,0:T(8,128)(2,1)S(1)}, u32[]{:S(2)}, u32[]{:S(2)}) collective-permute-start(bf16[2,96,384]{2,1,0:T(8,128)(2,1)S(1)} %get-tuple-element.108), channel_id=1, source_target_pairs={{0,8},{4,12},{8,0},{12,4},{16,24},{20,28},{24,16},{28,20},{1,9},{5... | collective-permute-start | bytes 442376 | tf_op jit(solution)/shard_map/ppermute | solution.py:25
  96.8 13.9 %collective-permute-start.28 = (bf16[2,96,384]{2,1,0:T(8,128)(2,1)S(1)}, bf16[2,96,384]{2,1,0:T(8,128)(2,1)S(1)}, u32[]{:S(2)}, u32[]{:S(2)}) collective-permute-start(bf16[2,96,384]{2,1,0:T(8,128)(2,1)S(1)} %get-tuple-element.109), channel_id=1, source_target_pairs={{0,4},{4,0},{8,12},{12,8},{16,20},{20,16},{24,28},{28,24},{1,5},{5... | collective-permute-start | bytes 442376 | tf_op jit(solution)/shard_map/ppermute | solution.py:25
  98.4 7.9 %collective-permute-start.18 = (bf16[400,128]{1,0:T(8,128)(2,1)S(1)}, bf16[400,128]{1,0:T(8,128)(2,1)S(1)}, u32[]{:S(2)}, u32[]{:S(2)}) collective-permute-start(bf16[400,128]{1,0:T(8,128)(2,1)S(1)} %get-tuple-element.86), channel_id=1, source_target_pairs={{0,8},{4,12},{8,0},{12,4},{16,24},{20,28},{24,16},{28,20},{1,9},{5... | collective-permute-start | bytes 307208 | tf_op jit(solution)/shard_map/ppermute | solution.py:25
  100.3 12.5 %collective-permute-start.19 = (bf16[400,128]{1,0:T(8,128)(2,1)S(1)}, bf16[400,128]{1,0:T(8,128)(2,1)S(1)}, u32[]{:S(2)}, u32[]{:S(2)}) collective-permute-start(bf16[400,128]{1,0:T(8,128)(2,1)S(1)} %get-tuple-element.87), channel_id=1, source_target_pairs={{0,12},{4,8},{8,4},{12,0},{16,28},{20,24},{24,20},{28,16},{1,13},{... | collective-permute-start | bytes 307208 | tf_op jit(solution)/shard_map/ppermute | solution.py:25
  101.8 16.8 %collective-permute-start.20 = (bf16[400,128]{1,0:T(8,128)(2,1)S(1)}, bf16[400,128]{1,0:T(8,128)(2,1)S(1)}, u32[]{:S(2)}, u32[]{:S(2)}) collective-permute-start(bf16[400,128]{1,0:T(8,128)(2,1)S(1)} %get-tuple-element.88), channel_id=1, source_target_pairs={{0,16},{4,20},{8,24},{12,28},{16,0},{20,4},{24,8},{28,12},{1,17},{... | collective-permute-start | bytes 307208 | tf_op jit(solution)/shard_map/ppermute | solution.py:25
  106.3 16.2 %collective-permute-start.21 = (bf16[400,128]{1,0:T(8,128)(2,1)S(1)}, bf16[400,128]{1,0:T(8,128)(2,1)S(1)}, u32[]{:S(2)}, u32[]{:S(2)}) collective-permute-start(bf16[400,128]{1,0:T(8,128)(2,1)S(1)} %get-tuple-element.89), channel_id=1, source_target_pairs={{0,20},{4,16},{8,28},{12,24},{16,4},{20,0},{24,12},{28,8},{1,21},{... | collective-permute-start | bytes 307208 | tf_op jit(solution)/shard_map/ppermute | solution.py:25
  108.1 14.4 %collective-permute-start.22 = (bf16[400,128]{1,0:T(8,128)(2,1)S(1)}, bf16[400,128]{1,0:T(8,128)(2,1)S(1)}, u32[]{:S(2)}, u32[]{:S(2)}) collective-permute-start(bf16[400,128]{1,0:T(8,128)(2,1)S(1)} %get-tuple-element.90), channel_id=1, source_target_pairs={{0,24},{4,28},{8,16},{12,20},{16,8},{20,12},{24,0},{28,4},{1,25},{... | collective-permute-start | bytes 307208 | tf_op jit(solution)/shard_map/ppermute | solution.py:25
  110.7 11.8 %collective-permute-start.23 = (bf16[400,128]{1,0:T(8,128)(2,1)S(1)}, bf16[400,128]{1,0:T(8,128)(2,1)S(1)}, u32[]{:S(2)}, u32[]{:S(2)}) collective-permute-start(bf16[400,128]{1,0:T(8,128)(2,1)S(1)} %get-tuple-element.91), channel_id=1, source_target_pairs={{0,28},{4,24},{8,20},{12,16},{16,12},{20,8},{24,4},{28,0},{1,29},{... | collective-permute-start | bytes 307208 | tf_op jit(solution)/shard_map/ppermute | solution.py:25
  112.8 14.8 %collective-permute-start.29 = (bf16[1,96,384]{2,1,0:T(8,128)(2,1)S(1)}, bf16[1,96,384]{2,1,0:T(8,128)(2,1)S(1)}, u32[]{:S(2)}, u32[]{:S(2)}) collective-permute-start(bf16[1,96,384]{2,1,0:T(8,128)(2,1)S(1)} %get-tuple-element.112), channel_id=1, source_target_pairs={{0,16},{4,20},{8,24},{12,28},{16,0},{20,4},{24,8},{28,12},{1,17},{... | collective-permute-start | bytes 221192 | tf_op jit(solution)/shard_map/ppermute | solution.py:25
  118.7 10.1 %collective-permute-start.30 = (bf16[1,96,384]{2,1,0:T(8,128)(2,1)S(1)}, bf16[1,96,384]{2,1,0:T(8,128)(2,1)S(1)}, u32[]{:S(2)}, u32[]{:S(2)}) collective-permute-start(bf16[1,96,384]{2,1,0:T(8,128)(2,1)S(1)} %get-tuple-element.113), channel_id=1, source_target_pairs={{0,16},{4,20},{8,24},{12,28},{16,0},{20,4},{24,8},{28,12},{1,17},{... | collective-permute-start | bytes 221192 | tf_op jit(solution)/shard_map/ppermute | solution.py:25
  (13 other events, 176.6 us)
